TPU v7x, 128 devices: a whole 4x4x4 slice. The times are simulated.
128 devices in a mesh: row: 16 (over y, z), col: 8 (over x, core).
Axes of the slice: x: 4, y: 4, z: 4, core: 2. Of those that a mesh axis runs over, the one named last changes fastest.
Arguments:
- kernel_rows: float32 [2, 16, 8, 64, 16384], P(None, 'row', 'col'), may hold values from -1 to 8, as said below
Outputs:
- factored: float32 [2, 16, 512, 4, 8, 512], P(None, 'row', None, None, 'col')
Inputs may be any that keep to these rules, and one draw needn't show every extreme that they name: `kernel_rows`: the matrix A that the rows make is symmetric and positive definite.
All inputs are finite; a program needn't handle non-finite values.
Results may differ from a plain program's by a relative error of at most 0.0001.
Values sent between devices are 32-bit elements; how exact they have to be, the bound alone decides.
A program may use at most 128 MiB of HBM per device.

v0:
```python
import jax
import jax.numpy as jnp
from jax import lax
from jax.sharding import PartitionSpec as P


def spread(block, axis, owner):
    block = jnp.where(lax.axis_index(axis) == owner, block, jnp.zeros_like(block))
    return lax.psum(block, axis)


def solve_rows(factor_tile, column):
    row_tiles, tile_size = (column.shape[0], column.shape[1])
    stacked = column.reshape(row_tiles * tile_size, tile_size)
    solved = jax.scipy.linalg.solve_triangular(factor_tile, stacked.T, lower=True)
    return solved.T.reshape(row_tiles, tile_size, tile_size)


def factor(tiles_here, panel_idx, grid_rows, grid_cols):
    row_at, col_at = (panel_idx // grid_rows, panel_idx // grid_cols)
    row_root, col_root = (panel_idx % grid_rows, panel_idx % grid_cols)
    column = tiles_here[:, :, col_at, :]
    diag_piece = tiles_here[row_at, :, col_at, :]
    diag_tile = spread(diag_piece, "row", row_root)
    factor_tile = jnp.linalg.cholesky(diag_tile)
    solved = spread(solve_rows(factor_tile, column), "col", col_root)
    return (factor_tile, solved)


def mirror(solved, grid_rows, grid_cols):
    pieces = []
    for copy_idx in range(grid_rows // grid_cols):
        root_row = lax.axis_index("col") + copy_idx * grid_cols
        pieces.append(spread(solved, "row", root_row))
    row_tiles, tile_size = (solved.shape[0], solved.shape[1])
    return jnp.stack(pieces, axis=1).reshape(-1, tile_size, tile_size)


def update(
    tiles_here, panel_idx, factor_tile, solved, col_factor, row_ids, col_ids, grid_rows, grid_cols
):
    left_part = jnp.where((row_ids > panel_idx)[:, None, None], solved, jnp.float32(0.0))
    right_part = jnp.where((col_ids > panel_idx)[:, None, None], col_factor, jnp.float32(0.0))
    tiles_here = tiles_here - jnp.einsum(
        "aur,bvr->aubv", left_part, right_part, precision=lax.Precision.HIGHEST
    )
    row_at, col_at = (panel_idx // grid_rows, panel_idx // grid_cols)
    row_root, col_root = (panel_idx % grid_rows, panel_idx % grid_cols)
    below_mask = (row_ids > panel_idx)[:, None, None]
    diag_mask = (row_ids == panel_idx)[:, None, None]
    col_values = jnp.where(
        below_mask, solved, jnp.where(diag_mask, factor_tile[None], jnp.float32(0.0))
    )
    owner_col = lax.axis_index("col") == col_root
    tiles_here = tiles_here.at[:, :, col_at, :].set(
        jnp.where(owner_col, col_values, tiles_here[:, :, col_at, :])
    )
    zero_mask = (lax.axis_index("row") == row_root) & (col_ids > panel_idx)
    tiles_here = tiles_here.at[row_at].set(
        jnp.where(zero_mask[None, :, None], jnp.float32(0.0), tiles_here[row_at])
    )
    return tiles_here


def shards(kernel_rows):
    grid_rows = lax.axis_size("row")
    grid_cols = lax.axis_size("col")
    row_tiles, sub_rows, mat_order = (
        kernel_rows.shape[0],
        kernel_rows.shape[3],
        kernel_rows.shape[4],
    )
    tile_size = sub_rows * grid_cols
    col_tiles = mat_order // (tile_size * grid_cols)
    shaped = kernel_rows.reshape(row_tiles, sub_rows, col_tiles, grid_cols, tile_size)
    placed = lax.all_to_all(shaped, "col", split_axis=3, concat_axis=1, tiled=True)
    tiles_here = placed.reshape(row_tiles, tile_size, col_tiles, tile_size)
    row_ids = jnp.arange(row_tiles, dtype=jnp.int32) * grid_rows + lax.axis_index("row")
    col_ids = jnp.arange(col_tiles, dtype=jnp.int32) * grid_cols + lax.axis_index("col")
    for panel_idx in range(2):
        factor_tile, solved = factor(tiles_here, panel_idx, grid_rows, grid_cols)
        col_factor = mirror(solved, grid_rows, grid_cols)
        tiles_here = update(
            tiles_here,
            panel_idx,
            factor_tile,
            solved,
            col_factor,
            row_ids,
            col_ids,
            grid_rows,
            grid_cols,
        )
    return tiles_here.reshape(row_tiles, 1, tile_size, col_tiles, 1, tile_size)


def solution(mesh):
    return jax.shard_map(
        shards,
        mesh=mesh,
        in_specs=(P(None, "row", "col", None, None),),
        out_specs=P(None, "row", None, None, "col", None),
        check_vma=False,
    )
```

profile of v0, /device:TPU:1, one launch (start us, length us, event | category | flops | bytes accessed | tf_op | source)
XLA Modules:
  0.0 1100.3 jit_solution(1424373501177448121)
XLA Ops:
  6.5 13.3 %copy.99 = f32[16,8,32,512]{3,2,1,0:T(8,128)} copy(f32[16,8,32,512]{3,1,2,0:T(8,128)} %bitcast.198) | data formatting | bytes 16777216
  19.8 23.6 %copy.63 = f32[2,64,4,8,512]{4,2,1,0,3:T(4,128)} copy(f32[2,64,4,8,512]{4,3,2,1,0:T(8,128)} %bitcast.197) | data formatting | bytes 16777216 | tf_op jit(solution)/shard_map/reshape | solution.py:75
  43.4 6.2 all-to-all-start
  49.6 93.7 %all-to-all-done = f32[2,64,4,8,512]{4,2,1,0,3:T(4,128)} async-done(((f32[2,64,4,8,512]{4,2,1,0,3:T(4,128)}), f32[2,64,4,8,512]{4,2,1,0,3:T(4,128)}, u32[]{:S(2)}, u32[]{:S(2)}) %all-to-all-start) | async-done | bytes 8388640 | tf_op jit(solution)/shard_map/all_to_all | solution.py:76
  159.2 82.0 %all-reduce.10.cloned.1.call-done = f32[512,512]{0,1:T(8,128)} async-done(((f32[512,512]{0,1:T(8,128)}), f32[512,512]{0,1:T(8,128)}) %all-reduce.10.cloned.1.call-update) | async-done | bytes 1048592 | tf_op jit(solution)/shard_map/psum | solution.py:9
  246.3 11.7 %cholesky.286 = f32[128,128]{1,0:T(8,128)S(1)} custom-call(f32[128,128]{1,0:T(8,128)S(1)} %cholesky.426), custom_call_target="Cholesky" | custom-call | tf_op jit(solution)/shard_map/jit(cholesky)/cholesky | solution.py:25
  258.1 9.8 custom-call.27
  270.6 11.7 %cholesky.305 = f32[128,128]{1,0:T(8,128)S(1)} custom-call(f32[128,128]{1,0:T(8,128)S(1)} %cholesky.430), custom_call_target="Cholesky" | custom-call | tf_op jit(solution)/shard_map/jit(cholesky)/cholesky | solution.py:25
  282.3 10.2 custom-call.28
  294.1 11.7 %cholesky.326 = f32[128,128]{1,0:T(8,128)S(1)} custom-call(f32[128,128]{1,0:T(8,128)S(1)} %cholesky.435), custom_call_target="Cholesky" | custom-call | tf_op jit(solution)/shard_map/jit(cholesky)/cholesky | solution.py:25
  306.5 9.8 custom-call.29
  317.8 11.7 %cholesky.343 = f32[128,128]{1,0:T(8,128)S(1)} custom-call(f32[128,128]{1,0:T(8,128)S(1)} %convolution_subtract_fusion.9), custom_call_target="Cholesky" | custom-call | tf_op jit(solution)/shard_map/jit(cholesky)/cholesky | solution.py:25
  335.3 11.7 %while.8 = (s32[]{:T(128)}, f32[512,512]{1,0:T(8,128)}, s32[4,2]{0,1:T(2,128)S(1)}, f32[4,128,128]{2,1,0:T(8,128)S(1)}, s32[]{:T(128)}) while((s32[]{:T(128)}, f32[512,512]{1,0:T(8,128)}, s32[4,2]{0,1:T(2,128)S(1)}, f32[4,128,128]{2,1,0:T(8,128)S(1)}, s32[]{:T(128)}) %tuple.74), condition=%wide.while_cond.4, body=%wide.while_body.4.sunk | while | flops 2 | bytes 131181 | solution.py:15
  347.0 39.3 %custom-call.30 = f32[4,128,128]{1,2,0:T(8,128)S(1)} custom-call(f32[4,128,128]{2,1,0:T(8,128)S(1)} %get-tuple-element.69), custom_call_target="InvertDiagBlocksLowerTriangular" | custom-call | tf_op jit(solution)/shard_map/jit(_solve_triangular)/triangular_solve | solution.py:15
  399.0 64.5 %all-reduce.12.cloned.1.call-done = f32[2,512,512]{1,2,0:T(8,128)} async-done(((f32[2,512,512]{1,2,0:T(8,128)}), f32[2,512,512]{1,2,0:T(8,128)}) %all-reduce.12.cloned.1.call-update) | async-done | bytes 2097168 | tf_op jit(solution)/shard_map/psum | solution.py:9
  467.9 10.2 copy.72
  478.4 94.4 %all-reduce.20.cloned.1.call-done = (f32[2,1,512,512]{2,3,0,1:T(8,128)}, f32[2,1,512,512]{2,3,0,1:T(8,128)}) async-done(((f32[2,1,512,512]{2,3,0,1:T(8,128)}, f32[2,1,512,512]{2,3,0,1:T(8,128)}), (f32[2,1,512,512]{2,3,0,1:T(8,128)}, f32[2,1,512,512]{2,3,0,1:T(8,128)})) %all-reduce.20.cloned.1.call-update) | async-done | bytes 4194320 | tf_op jit(solution)/shard_map/psum | solution.py:9
  585.9 18.0 %fusion.10 = f32[2,512,4,512]{1,3,0,2:T(8,128)S(1)} fusion(f32[2,512,4,512]{1,3,0,2:T(8,128)} %copy.72, f32[4,512,512]{2,1,0:T(8,128)S(1)} %bitcast_select_fusion.1, f32[2,512,512]{1,2,0:T(8,128)S(1)} %copy-done.1, pred[2]{0:T(512)(128)(4,1)S(1)} %get-tuple-element.130), kind=kOutput, calls=%fused_computation.18 | convolution fusion | flops 12887523328 | bytes 23068674 | tf_op jit(solution)/shard_map/aur,bvr->aubv/dot_general | solution.py:44
  622.5 80.2 %all-reduce.14.cloned.1.call-done = f32[512,512]{0,1:T(8,128)} async-done(((f32[512,512]{0,1:T(8,128)}), f32[512,512]{0,1:T(8,128)}) %all-reduce.14.cloned.1.call-update) | async-done | bytes 1048592 | tf_op jit(solution)/shard_map/psum | solution.py:9
  707.9 11.7 %cholesky.358 = f32[128,128]{1,0:T(8,128)S(1)} custom-call(f32[128,128]{1,0:T(8,128)S(1)} %cholesky.439), custom_call_target="Cholesky" | custom-call | tf_op jit(solution)/shard_map/jit(cholesky)/cholesky | solution.py:25
  719.7 9.8 custom-call.31
  732.1 11.7 %cholesky.377 = f32[128,128]{1,0:T(8,128)S(1)} custom-call(f32[128,128]{1,0:T(8,128)S(1)} %cholesky.443), custom_call_target="Cholesky" | custom-call | tf_op jit(solution)/shard_map/jit(cholesky)/cholesky | solution.py:25
  745.2 10.0 custom-call.32
  756.7 11.7 %cholesky.398 = f32[128,128]{1,0:T(8,128)S(1)} custom-call(f32[128,128]{1,0:T(8,128)S(1)} %cholesky.448), custom_call_target="Cholesky" | custom-call | tf_op jit(solution)/shard_map/jit(cholesky)/cholesky | solution.py:25
  769.1 9.8 custom-call.33
  780.4 11.7 %cholesky.415 = f32[128,128]{1,0:T(8,128)S(1)} custom-call(f32[128,128]{1,0:T(8,128)S(1)} %convolution_subtract_fusion.8), custom_call_target="Cholesky" | custom-call | tf_op jit(solution)/shard_map/jit(cholesky)/cholesky | solution.py:25
  797.2 11.7 %while.9 = (s32[]{:T(128)}, f32[512,512]{1,0:T(8,128)}, s32[4,2]{0,1:T(2,128)S(1)}, f32[4,128,128]{2,1,0:T(8,128)S(1)}, s32[]{:T(128)}) while((s32[]{:T(128)}, f32[512,512]{1,0:T(8,128)}, s32[4,2]{0,1:T(2,128)S(1)}, f32[4,128,128]{2,1,0:T(8,128)S(1)}, s32[]{:T(128)}) %tuple.94), condition=%wide.while_cond.4.clone, body=%wide.while_body.4.clone.sunk | while | flops 2 | bytes 131181 | solution.py:15
  809.0 39.3 %custom-call.34 = f32[4,128,128]{1,2,0:T(8,128)S(1)} custom-call(f32[4,128,128]{2,1,0:T(8,128)S(1)} %get-tuple-element.70), custom_call_target="InvertDiagBlocksLowerTriangular" | custom-call | tf_op jit(solution)/shard_map/jit(_solve_triangular)/triangular_solve | solution.py:15
  861.0 64.4 %all-reduce.16.cloned.1.call-done = f32[2,512,512]{1,2,0:T(8,128)} async-done(((f32[2,512,512]{1,2,0:T(8,128)}), f32[2,512,512]{1,2,0:T(8,128)}) %all-reduce.16.cloned.1.call-update) | async-done | bytes 2097168 | tf_op jit(solution)/shard_map/psum | solution.py:9
  931.2 103.5 %all-reduce.18.cloned.1.call-done = (f32[2,1,512,512]{2,3,0,1:T(8,128)}, f32[2,1,512,512]{2,3,0,1:T(8,128)}) async-done(((f32[2,1,512,512]{2,3,0,1:T(8,128)}, f32[2,1,512,512]{2,3,0,1:T(8,128)}), (f32[2,1,512,512]{2,3,0,1:T(8,128)}, f32[2,1,512,512]{2,3,0,1:T(8,128)})) %all-reduce.18.cloned.1.call-update) | async-done | bytes 4194320 | tf_op jit(solution)/shard_map/psum | solution.py:9
  1047.9 18.0 %fusion.7 = f32[2,512,4,512]{1,3,2,0:T(8,128)S(1)} fusion(f32[2,512,4,512]{1,3,2,0:T(8,128)} %get-tuple-element.93, f32[4,512,512]{2,1,0:T(8,128)S(1)} %bitcast_select_fusion, f32[2,512,512]{1,2,0:T(8,128)S(1)} %copy-done.2, pred[2]{0:T(512)(128)(4,1)S(1)} %get-tuple-element.132), kind=kOutput, calls=%fused_computation.17 | convolution fusion | flops 12887523328 | bytes 23068674 | tf_op jit(solution)/shard_map/aur,bvr->aubv/dot_general | solution.py:44
  1072.5 20.5 %copy.88 = f32[2,1,512,4,1,512]{5,4,3,2,1,0:T(1,128)} copy(f32[2,1,512,4,1,512]{2,5,3,0,4,1:T(8,128)} %fusion.2) | data formatting | bytes 16777216 | tf_op jit(solution)/shard_map/scatter | solution.py:59
  (151 shorter events, 156.2 us)
Async XLA Ops:
  43.4 100.0 %all-to-all-start = ((f32[2,64,4,8,512]{4,2,1,0,3:T(4,128)}), f32[2,64,4,8,512]{4,2,1,0,3:T(4,128)}, u32[]{:S(2)}, u32[]{:S(2)}) async-start(f32[2,64,4,8,512]{4,2,1,0,3:T(4,128)} %copy.63), calls=%async_computation | async-start | bytes 16777216 | tf_op jit(solution)/shard_map/all_to_all | solution.py:76
  49.6 191.6 %all-reduce.10.cloned.1.call-start = ((), (), s32[]{:S(2)}) async-start(), calls=%async_computation.1 | async-start | bytes 2097152 | tf_op jit(solution)/shard_map/psum | solution.py:9
  149.2 3.4 copy-start
  154.1 309.3 %all-reduce.12.cloned.1.call-start = ((), (), s32[]{:S(2)}) async-start(), calls=%async_computation.2 | async-start | bytes 4194304 | tf_op jit(solution)/shard_map/psum | solution.py:9
  241.2 2.6 copy-start.3
  245.3 1.0 copy-start.8
  398.9 173.9 %all-reduce.20.cloned.1.call-start = ((), (), s32[]{:S(2)}) async-start(), calls=%async_computation.6 | async-start | bytes 8388608 | tf_op jit(solution)/shard_map/psum | solution.py:9
  467.8 235.0 %all-reduce.14.cloned.1.call-start = ((), (), s32[]{:S(2)}) async-start(), calls=%async_computation.3 | async-start | bytes 2097152 | tf_op jit(solution)/shard_map/psum | solution.py:9
  467.9 10.2 copy-start.5
  582.7 3.2 copy-start.1
  616.4 309.0 %all-reduce.16.cloned.1.call-start = ((), (), s32[]{:S(2)}) async-start(), calls=%async_computation.4 | async-start | bytes 4194304 | tf_op jit(solution)/shard_map/psum | solution.py:9
  702.8 2.6 copy-start.4
  706.8 1.0 copy-start.7
  860.9 173.8 %all-reduce.18.cloned.1.call-start = ((), (), s32[]{:S(2)}) async-start(), calls=%async_computation.5 | async-start | bytes 8388608 | tf_op jit(solution)/shard_map/psum | solution.py:9
  929.6 1.2 copy-start.6
  1044.7 3.2 copy-start.2
Sparse Core Ops, SparseCore 0:
  154.2 86.9 all-reduce.9
  399.0 64.3 all-reduce.11
  467.9 104.8 all-reduce.19
  616.5 86.1 all-reduce.13
  861.0 64.2 all-reduce.15
  929.8 104.8 all-reduce.17
where the time goes:
time: 1110 us; the launch traced here: 1100 us
  waiting for transfers between devices  583 us (53%)
  other arithmetic  280 us (25%)
  local copies, waits for them, and re-layouts  149 us (13%)
  matrix products  62.2 us (6%)
  between operations  19.6 us (2%)
    psum x6, waiting for transfers between devices, spread(): return lax.psum(block, axis)  489 us
    another operation x29, other arithmetic, factor(): factor_tile = jnp.linalg.cholesky(diag_tile)  158 us
    all_to_all x1, waiting for transfers between devices, shards(): lax.all_to_all(shaped, 'col', split_axis=3, concat_axis=1, tiled=True)  93.7 us
    another operation x5, other arithmetic, solve_rows(): jax.scipy.linalg.solve_triangular(factor_tile, stacked.T, lower=True)  82.2 us
    dot_general x2, matrix products, update(): jnp.einsum('aur,bvr->aubv', left_part, right_part, precision=lax.Precisio...  36 us
    reshape x1, local copies, waits for them, and re-layouts, shards(): kernel_rows.reshape(row_tiles, sub_rows, col_tiles, grid_cols, tile_size)  23.6 us
    unnamed x21, local copies, waits for them, and re-layouts  23.4 us
    another operation x27, local copies, waits for them, and re-layouts, solve_rows(): jax.scipy.linalg.solve_triangular(factor_tile, stacked.T, lower=True)  23.3 us
  transfers between devices with their start and end apart: 7, of which 7 were waited for; matrix products, arithmetic and copies ran while one was open for 2% of the time, Pallas kernels for 0%

commit v1 on v0

v1 whole, which is shorter than its diff:
```python
import functools
import jax
import jax.numpy as jnp
from jax import lax
from jax.experimental import pallas as pl
from jax.experimental.pallas import tpu as pltpu
from jax.sharding import PartitionSpec as P

MESH = pl.DeviceIdType.MESH
HI = lax.Precision.HIGHEST
F32 = jnp.float32
BF16 = jnp.bfloat16
BLK = 128
STRIP = 8
VMEM_CAP = 64 * 1024 * 1024 - 128 * 1024


def rcopy(src, dst, ssem, rsem, row, col):
    return pltpu.make_async_remote_copy(
        src_ref=src, dst_ref=dst, send_sem=ssem, recv_sem=rsem,
        device_id=(row, col), device_id_type=MESH)


def wait_for(ref, sem):
    pltpu.make_async_copy(ref, ref, sem).wait()


def comm_kernel(kr, tiles, panels, head, slab, own, ssem, rsem, lsem):
    g = lax.axis_index("row")
    c = lax.axis_index("col")
    core = lax.rem(c, 2)
    chip = c // 2
    swap_row = (g // 8) * 8 + c
    swap_col = lax.rem(g, 8)
    is_self = swap_col == c
    slot = 2 + g // 8
    sub = pl.multiple_of(lax.rem(g, 8) * 64, 64)
    mine = pl.multiple_of(c * 64, 64)

    pltpu.make_async_copy(kr.at[:, :, pl.ds(0, 1024)], slab, lsem.at[0]).start()
    for a in range(2):
        for b in range(4):
            at = pl.multiple_of((b * 8 + c) * 512, 512)
            pltpu.make_async_copy(
                kr.at[a, :, pl.ds(at, 512)], own.at[a, b], lsem.at[1]).start()

    barrier = pltpu.get_barrier_semaphore()

    @pl.loop(1, 16)
    def _(o):
        pl.semaphore_signal(barrier, inc=1, device_id=(lax.rem(g + o, 16), c), device_id_type=MESH)

    @pl.loop(1, 8)
    def _(o):
        pl.semaphore_signal(barrier, inc=1, device_id=(g, lax.rem(c + o, 8)), device_id_type=MESH)

    @pl.when(jnp.logical_not(is_self))
    def _():
        pl.semaphore_signal(barrier, inc=1, device_id=(swap_row, swap_col), device_id_type=MESH)
        pl.semaphore_wait(barrier, 23)

    @pl.when(is_self)
    def _():
        pl.semaphore_wait(barrier, 22)

    wait_for(slab, lsem.at[0])

    for a in range(2):
        for o in range(1, 4):
            rcopy(slab.at[a], panels.at[a, pl.ds(mine, 64), :], ssem.at[a], rsem.at[a],
                  g, lax.rem(c + 2 * o, 8)).start()
        rcopy(slab.at[a], panels.at[a, pl.ds(mine, 64), :], ssem.at[2], rsem.at[2],
              g, chip * 2 + 1 - core).start()
        pltpu.make_async_copy(slab.at[a], panels.at[a, pl.ds(mine, 64), :], lsem.at[2]).start()

    @pl.when(jnp.logical_not(is_self))
    def _():
        for a in range(2):
            rcopy(slab.at[a], panels.at[2 + g // 8 + 2 * a, pl.ds(mine, 64), :],
                  ssem.at[3], rsem.at[3], swap_row, swap_col).start()

    @pl.when(is_self)
    def _():
        for a in range(2):
            pltpu.make_async_copy(
                slab.at[a], panels.at[slot + 2 * a, pl.ds(sub, 64), :], lsem.at[3]).start()

    @pl.loop(1, 8)
    def _(o):
        cc = lax.rem(c + o, 8)
        for a in range(2):
            for b in range(4):
                at = pl.multiple_of((b * 8 + cc) * 512, 512)
                rcopy(kr.at[a, :, pl.ds(at, 512)], tiles.at[a, b, pl.ds(mine, 64), :],
                      ssem.at[4], rsem.at[4], g, cc).start()

    wait_for(own, lsem.at[1])
    for a in range(2):
        for b in range(4):
            pltpu.make_async_copy(
                own.at[a, b], tiles.at[a, b, pl.ds(mine, 64), :], lsem.at[4]).start()

    wait_for(panels.at[0, pl.ds(0, 192), :], rsem.at[0])
    wait_for(slab, lsem.at[2])

    def piece_row(q):
        return pl.multiple_of((2 * (q // 4) + core) * 64 + lax.rem(q, 4) * 16, 16)

    def scatter(root, lanes_at, lanes, index):
        @pl.when(g == root)
        def _():
            @pl.loop(1, 16)
            def _(o):
                q = lax.rem(g + o, 16)
                r = piece_row(q)
                rcopy(panels.at[0, pl.ds(r, 16), pl.ds(lanes_at, lanes)],
                      head.at[pl.ds(root * 512 + r, 16), pl.ds(lanes_at, lanes)],
                      ssem.at[5 + index], rsem.at[5 + index], q, c).start()
            r = piece_row(g)
            cp = pltpu.make_async_copy(
                panels.at[0, pl.ds(r, 16), pl.ds(lanes_at, lanes)],
                head.at[pl.ds(root * 512 + r, 16), pl.ds(lanes_at, lanes)], lsem.at[5])
            cp.start()
            cp.wait()

        @pl.when(g != root)
        def _():
            wait_for(head.at[pl.ds(0, 16), pl.ds(lanes_at, lanes)], rsem.at[5 + index])

    def gather(root, lanes_at, lanes, index):
        r = piece_row(g)
        src = head.at[pl.ds(root * 512 + r, 16), pl.ds(lanes_at, lanes)]

        @pl.loop(1, 16)
        def _(o):
            rcopy(src, src, ssem.at[7 + index], rsem.at[7 + index], lax.rem(g + o, 16), c).start()

    def swap(root, lanes_at, lanes, index):
        wait_for(head.at[pl.ds(0, 240), pl.ds(lanes_at, lanes)], rsem.at[7 + index])
        for m in range(4):
            r = pl.multiple_of(root * 512 + (2 * m + core) * 64, 64)
            src = head.at[pl.ds(r, 64), pl.ds(lanes_at, lanes)]
            rcopy(src, src, ssem.at[9 + index], rsem.at[9 + index], g, chip * 2 + 1 - core).start()

    scatter(0, 0, 1024, 0)
    scatter(1, 512, 512, 1)
    gather(0, 0, 1024, 0)
    gather(1, 512, 512, 1)

    @pl.when(jnp.logical_not(is_self))
    def _():
        wait_for(panels.at[0, pl.ds(0, 128), :], rsem.at[3])

    @pl.when(is_self)
    def _():
        wait_for(slab, lsem.at[3])

    @pl.loop(1, 16)
    def _(o):
        q = lax.rem(g + o, 16)
        for a in range(2):
            src = panels.at[slot + 2 * a, pl.ds(sub, 64), :]
            rcopy(src, src, ssem.at[11], rsem.at[11], q, c).start()

    swap(0, 0, 1024, 0)
    swap(1, 512, 512, 1)

    wait_for(panels.at[0, pl.ds(0, 192), :], rsem.at[1])
    for a in range(2):
        for o in range(1, 4):
            at = pl.multiple_of(lax.rem(c + 2 * o, 8) * 64, 64)
            src = panels.at[a, pl.ds(at, 64), :]
            rcopy(src, src, ssem.at[12], rsem.at[12], g, chip * 2 + 1 - core).start()

    wait_for(head.at[pl.ds(0, 256), :], rsem.at[9])
    wait_for(head.at[pl.ds(0, 256), pl.ds(512, 512)], rsem.at[10])
    wait_for(panels.at[0, pl.ds(0, 128), :], rsem.at[2])
    wait_for(panels.at[0, pl.ds(0, 384), :], rsem.at[12])
    wait_for(panels.at[pl.ds(0, 4), pl.ds(0, 480), :], rsem.at[11])
    wait_for(own, lsem.at[4])
    wait_for(tiles.at[:, :, pl.ds(0, 448), :], rsem.at[4])
    wait_for(panels.at[0, pl.ds(0, 192), :], ssem.at[0])
    wait_for(panels.at[0, pl.ds(0, 192), :], ssem.at[1])
    wait_for(panels.at[0, pl.ds(0, 128), :], ssem.at[2])

    @pl.when(jnp.logical_not(is_self))
    def _():
        wait_for(panels.at[0, pl.ds(0, 128), :], ssem.at[3])

    wait_for(tiles.at[:, :, pl.ds(0, 448), :], ssem.at[4])

    @pl.when(g == 0)
    def _():
        wait_for(head.at[pl.ds(0, 240), :], ssem.at[5])

    @pl.when(g == 1)
    def _():
        wait_for(head.at[pl.ds(0, 240), pl.ds(512, 512)], ssem.at[6])

    wait_for(head.at[pl.ds(0, 240), :], ssem.at[7])
    wait_for(head.at[pl.ds(0, 240), pl.ds(512, 512)], ssem.at[8])
    wait_for(head.at[pl.ds(0, 256), :], ssem.at[9])
    wait_for(head.at[pl.ds(0, 256), pl.ds(512, 512)], ssem.at[10])
    wait_for(panels.at[pl.ds(0, 4), pl.ds(0, 480), :], ssem.at[11])
    wait_for(panels.at[0, pl.ds(0, 384), :], ssem.at[12])


def exchange(rows):
    anyspace = pl.BlockSpec(memory_space=pl.ANY)
    return pl.pallas_call(
        comm_kernel,
        out_shape=(
            jax.ShapeDtypeStruct((2, 4, 512, 512), F32),
            jax.ShapeDtypeStruct((6, 512, 1024), F32),
            jax.ShapeDtypeStruct((1024, 1024), F32),
        ),
        in_specs=[anyspace],
        out_specs=(anyspace, anyspace, anyspace),
        scratch_shapes=[
            pltpu.VMEM((2, 64, 1024), F32),
            pltpu.VMEM((2, 4, 64, 512), F32),
            pltpu.SemaphoreType.DMA((13,)),
            pltpu.SemaphoreType.DMA((13,)),
            pltpu.SemaphoreType.DMA((6,)),
        ],
        compiler_params=pltpu.CompilerParams(collective_id=1, has_side_effects=True),
        name="exchange",
    )(rows)


def dot_tn(lhs, rhs):
    return lax.dot_general(lhs, rhs, (((0,), (0,)), ((), ())), precision=HI,
                           preferred_element_type=F32)


def factor_block(block):
    count = BLK // STRIP
    lane = lax.broadcasted_iota(jnp.int32, (STRIP, BLK), 1)
    sublane = lax.broadcasted_iota(jnp.int32, (STRIP, BLK), 0)
    left = [block[STRIP * t:STRIP * (t + 1), :] for t in range(count)]
    right = [jnp.where(lane == sublane + STRIP * t, F32(1.0), F32(0.0)) for t in range(count)]
    upper, inverse = [], []
    for t in range(count):
        row = [jnp.broadcast_to(left[t][i:i + 1, :], (STRIP, BLK)) for i in range(STRIP)]
        inv = [jnp.broadcast_to(right[t][i:i + 1, :], (STRIP, BLK)) for i in range(STRIP)]
        entry = {}
        for i in range(STRIP):
            for j in range(i, STRIP):
                at = STRIP * t + j
                entry[i, j] = jnp.broadcast_to(row[i][:, at:at + 1], (STRIP, BLK))
        for k in range(STRIP):
            scale = lax.rsqrt(entry[k, k])
            row[k] = row[k] * scale
            inv[k] = inv[k] * scale
            factor = {i: entry[k, i] * scale for i in range(k + 1, STRIP)}
            for i in range(k + 1, STRIP):
                for j in range(i, STRIP):
                    entry[i, j] = entry[i, j] - factor[i] * factor[j]
                row[i] = row[i] - factor[i] * row[k]
                inv[i] = inv[i] - factor[i] * inv[k]
        strip_row, strip_inv = row[0], inv[0]
        for i in range(1, STRIP):
            strip_row = jnp.where(sublane == i, row[i], strip_row)
            strip_inv = jnp.where(sublane == i, inv[i], strip_inv)
        strip_row = jnp.where(lane >= sublane + STRIP * t, strip_row, F32(0.0))
        upper.append(strip_row)
        inverse.append(strip_inv)
        if t + 1 < count:
            change = dot_tn(strip_row, jnp.concatenate([strip_row, strip_inv], axis=1))
            for s in range(t + 1, count):
                left[s] = left[s] - change[STRIP * s:STRIP * (s + 1), :BLK]
                right[s] = right[s] - change[STRIP * s:STRIP * (s + 1), BLK:]
    return jnp.concatenate(upper, axis=0), jnp.concatenate(inverse, axis=0)


def factor_kernel(head, lower, winv, work, diag):
    work[...] = head[...]
    blocks = 1024 // BLK
    lane_blk = lax.broadcasted_iota(jnp.int32, (BLK, 1024), 1) // BLK

    @pl.loop(0, blocks)
    def _(kb):
        at = pl.multiple_of(kb * BLK, BLK)
        upper, inverse = factor_block(work[pl.ds(at, BLK), pl.ds(at, BLK)])
        diag[kb] = upper
        strip = jnp.dot(inverse, work[pl.ds(at, BLK), :], precision=HI, preferred_element_type=F32)
        work[pl.ds(at, BLK), :] = strip
        work[pl.ds(at, BLK), pl.ds(at, BLK)] = inverse

        @pl.loop(kb + 1, blocks)
        def _(rb):
            to = pl.multiple_of(rb * BLK, BLK)
            change = dot_tn(work[pl.ds(at, BLK), pl.ds(to, BLK)], work[pl.ds(at, BLK), :])
            old = work[pl.ds(to, BLK), :]
            work[pl.ds(to, BLK), :] = jnp.where(lane_blk == kb, F32(0.0), old) - change

    for r in range(blocks):
        winv[r * BLK:(r + 1) * BLK, :] = jnp.where(
            lane_blk <= r, work[r * BLK:(r + 1) * BLK, :], F32(0.0))
    lower[...] = jnp.zeros_like(lower)
    for r in range(blocks):
        for s in range(r + 1):
            which = (r // 4) + (s // 4)
            src = diag[r] if r == s else work[s * BLK:(s + 1) * BLK, r * BLK:(r + 1) * BLK]
            lower[which, (r % 4) * BLK:(r % 4 + 1) * BLK, (s % 4) * BLK:(s % 4 + 1) * BLK] = src.T


def factorize(head):
    return pl.pallas_call(
        factor_kernel,
        out_shape=(
            jax.ShapeDtypeStruct((3, 512, 512), F32),
            jax.ShapeDtypeStruct((1024, 1024), F32),
        ),
        scratch_shapes=[pltpu.VMEM((1024, 1024), F32), pltpu.VMEM((8, BLK, BLK), F32)],
        compiler_params=pltpu.CompilerParams(vmem_limit_bytes=40 * 1024 * 1024),
        name="factorize",
    )(head)


def halves(x):
    high = x.astype(BF16)
    return high, (x - high.astype(F32)).astype(BF16)


def dot_nt3(lhs, rhs):
    def one(p, q):
        return lax.dot_general(p, q, (((1,), (1,)), ((), ())), preferred_element_type=F32)
    return one(lhs[0], rhs[0]) + (one(lhs[0], rhs[1]) + one(lhs[1], rhs[0]))


def solve_kernel(panel, winv, high, low, whigh, wlow):
    @pl.when(pl.program_id(0) == 0)
    def _():
        top, rest = halves(winv[...])
        whigh[...] = top
        wlow[...] = rest

    top, rest = halves(panel[0])
    first = dot_nt3((top[:, :512], rest[:, :512]), (whigh[:512, :512], wlow[:512, :512]))
    second = dot_nt3((top, rest), (whigh[512:, :], wlow[512:, :]))
    high[0, :, :512], low[0, :, :512] = halves(first)
    high[0, :, 512:], low[0, :, 512:] = halves(second)


def solve_panels(panels, winv):
    block = pl.BlockSpec((1, 512, 1024), lambda i: (i, 0, 0))
    return pl.pallas_call(
        solve_kernel,
        grid=(6,),
        out_shape=(jax.ShapeDtypeStruct((6, 512, 1024), BF16),) * 2,
        in_specs=[block, pl.BlockSpec((1024, 1024), lambda i: (0, 0))],
        out_specs=(block, block),
        scratch_shapes=[pltpu.VMEM((1024, 1024), BF16)] * 2,
        compiler_params=pltpu.CompilerParams(vmem_limit_bytes=40 * 1024 * 1024),
        name="solve",
    )(panels, winv)


def update_kernel(tiles, high_row, low_row, high_col, low_col, lower, out):
    g = lax.axis_index("row")
    c = lax.axis_index("col")
    a, half = pl.program_id(0), pl.program_id(1)
    flat = out.at[0].reshape(512 * 8, 128)
    left = (high_row[0], low_row[0])

    def put(slot, value):
        for n in range(4):
            flat[pl.ds(slot * 4 + n, 512, stride=8), :] = value[:, n * 128:(n + 1) * 128]

    for b in range(2):
        put(b, tiles[0, b] - dot_nt3(left, (high_col[b], low_col[b])))

    @pl.when((half == 0) & (c == 0))
    def _():
        put(0, high_row[0, :, :512].astype(F32) + low_row[0, :, :512].astype(F32))

    @pl.when((half == 0) & (c == 1))
    def _():
        put(0, high_row[0, :, 512:].astype(F32) + low_row[0, :, 512:].astype(F32))

    @pl.when((a == 0) & (g < 2))
    def _():
        flat[...] = jnp.zeros((512 * 8, 128), F32)

        @pl.when((half == 0) & (c <= g))
        def _():
            put(0, lower[g + c])


def update_tiles(tiles, high, low, lower):
    row_block = pl.BlockSpec((1, 512, 1024), lambda a, h: (a, 0, 0))
    col_block = pl.BlockSpec((2, 512, 1024), lambda a, h: (1 + h, 0, 0))
    return pl.pallas_call(
        update_kernel,
        grid=(2, 2),
        out_shape=jax.ShapeDtypeStruct((2, 512, 16, 128), F32),
        in_specs=[
            pl.BlockSpec((1, 2, 512, 512), lambda a, h: (a, h, 0, 0)),
            row_block, row_block, col_block, col_block,
            pl.BlockSpec((3, 512, 512), lambda a, h: (0, 0, 0)),
        ],
        out_specs=pl.BlockSpec((1, 512, 8, 128), lambda a, h: (a, 0, h, 0)),
        compiler_params=pltpu.CompilerParams(vmem_limit_bytes=56 * 1024 * 1024),
        name="update",
    )(tiles, high, low, high, low, lower)


def shards(kernel_rows):
    rows = kernel_rows.reshape(2, 64, 16384)
    tiles, panels, head = exchange(rows)
    lower, winv = factorize(head)
    high, low = solve_panels(panels, winv)
    out = update_tiles(tiles, high, low, lower)
    return out.reshape(2, 1, 512, 4, 1, 512)


def solution(mesh):
    return jax.shard_map(
        shards,
        mesh=mesh,
        in_specs=(P(None, "row", "col", None, None),),
        out_specs=P(None, "row", None, None, "col", None),
        check_vma=False,
    )
```

time: 1110 us -> 418 us (0.38)
  the two profiles are of different devices: /device:TPU:1 before, /device:TPU:112 now
where the time goes in v1:
time: 418 us
  Pallas kernels  412 us (99%)
  local copies, waits for them, and re-layouts  6.56 us (2%)
    pallas_call x1, Pallas kernels, exchange(): pl.pallas_call(comm_kernel, out_shape=(jax.ShapeDtypeStruct((2, 4, 512, 5...  277 us
    pallas_call x1, Pallas kernels, factorize(): pl.pallas_call(factor_kernel, out_shape=(jax.ShapeDtypeStruct((3, 512, 51...  93.6 us
    pallas_call x1, Pallas kernels, update_tiles(): pl.pallas_call(update_kernel, grid=(2, 2), out_shape=jax.ShapeDtypeStruct...  22 us
    pallas_call x1, Pallas kernels, solve_panels(): pl.pallas_call(solve_kernel, grid=(6,), out_shape=(jax.ShapeDtypeStruct((...  19 us

profile of v1, /device:TPU:112, one launch (start us, length us, event | category | flops | bytes accessed | tf_op | source)
XLA Modules:
  0.0 418.2 jit_solution(17424010921887502798)
XLA Ops:
  0.0 277.0 %exchange.1 = (f32[2,4,512,512]{3,2,1,0:T(8,128)}, f32[6,512,1024]{2,1,0:T(8,128)}, f32[1024,1024]{1,0:T(8,128)}) custom-call(f32[2,64,16384]{2,1,0:T(8,128)} %bitcast.2), custom_call_target="tpu_custom_call" | custom-call | tf_op jit(solution)/shard_map/exchange/pallas_call | solution.py:210
  277.0 0.0 copy-start.1
  277.0 2.2 copy-done.1
  279.2 93.6 %factorize.1 = (f32[3,512,512]{2,1,0:T(8,128)S(1)}, f32[1024,1024]{1,0:T(8,128)S(1)}) custom-call(f32[1024,1024]{1,0:T(8,128)S(1)} %copy-done.1), custom_call_target="tpu_custom_call" | custom-call | tf_op jit(solution)/shard_map/factorize/pallas_call | solution.py:309
  372.8 0.0 copy-start.2
  372.8 1.7 copy-done.2
  374.5 19.0 %solve.1 = (bf16[6,512,1024]{2,1,0:T(8,128)(2,1)S(1)}, bf16[6,512,1024]{2,1,0:T(8,128)(2,1)}) custom-call(f32[6,512,1024]{2,1,0:T(8,128)} %get-tuple-element.13.panel, f32[1024,1024]{1,0:T(8,128)S(1)} %get-tuple-element.15.winv), custom_call_target="tpu_custom_call" | custom-call | tf_op jit(solution)/shard_map/solve/pallas_call | solution.py:348
  393.6 0.0 copy-start
  393.6 2.6 copy-done
  396.2 22.0 %update.1 = f32[2,512,16,128]{3,2,1,0:T(8,128)} custom-call(f32[2,4,512,512]{3,2,1,0:T(8,128)} %get-tuple-element.12.tiles, bf16[6,512,1024]{2,1,0:T(8,128)(2,1)} %copy-done, bf16[6,512,1024]{2,1,0:T(8,128)(2,1)} %get-tuple-element.17.low_row.low_col, bf16[6,512,1024]{2,1,0:T(8,128)(2,1)} %copy-done, ...), custom_call_target="tpu_custom_call" | custom-call | tf_op jit(solution)/shard_map/update/pallas_call | solution.py:394
Async XLA Ops:
  277.0 2.2 copy-start.1
  372.8 1.7 copy-start.2
  393.6 2.6 copy-start

commit v2 on v0

v2 whole, which is shorter than its diff:
```python
import functools
import jax
import jax.numpy as jnp
from jax import lax
from jax.experimental import pallas as pl
from jax.experimental.pallas import tpu as pltpu
from jax.sharding import PartitionSpec as P

MESH = pl.DeviceIdType.MESH
HI = lax.Precision.HIGHEST
F32 = jnp.float32
BF16 = jnp.bfloat16
BLK = 128
STRIP = 8
VMEM_CAP = 64 * 1024 * 1024 - 128 * 1024


def dot_tn(lhs, rhs):
    return lax.dot_general(lhs, rhs, (((0,), (0,)), ((), ())), precision=HI,
                           preferred_element_type=F32)


def factor_block(block):
    count = BLK // STRIP
    lane = lax.broadcasted_iota(jnp.int32, (STRIP, BLK), 1)
    sublane = lax.broadcasted_iota(jnp.int32, (STRIP, BLK), 0)
    left = [block[STRIP * t:STRIP * (t + 1), :] for t in range(count)]
    right = [jnp.where(lane == sublane + STRIP * t, F32(1.0), F32(0.0)) for t in range(count)]
    upper, inverse = [], []
    for t in range(count):
        row = [jnp.broadcast_to(left[t][i:i + 1, :], (STRIP, BLK)) for i in range(STRIP)]
        inv = [jnp.broadcast_to(right[t][i:i + 1, :], (STRIP, BLK)) for i in range(STRIP)]
        entry = {}
        for i in range(STRIP):
            for j in range(i, STRIP):
                at = STRIP * t + j
                entry[i, j] = jnp.broadcast_to(row[i][:, at:at + 1], (STRIP, BLK))
        for k in range(STRIP):
            scale = lax.rsqrt(entry[k, k])
            row[k] = row[k] * scale
            inv[k] = inv[k] * scale
            factor = {i: entry[k, i] * scale for i in range(k + 1, STRIP)}
            for i in range(k + 1, STRIP):
                for j in range(i, STRIP):
                    entry[i, j] = entry[i, j] - factor[i] * factor[j]
                row[i] = row[i] - factor[i] * row[k]
                inv[i] = inv[i] - factor[i] * inv[k]
        strip_row, strip_inv = row[0], inv[0]
        for i in range(1, STRIP):
            strip_row = jnp.where(sublane == i, row[i], strip_row)
            strip_inv = jnp.where(sublane == i, inv[i], strip_inv)
        strip_row = jnp.where(lane >= sublane + STRIP * t, strip_row, F32(0.0))
        upper.append(strip_row)
        inverse.append(strip_inv)
        if t + 1 < count:
            change = dot_tn(strip_row, jnp.concatenate([strip_row, strip_inv], axis=1))
            for s in range(t + 1, count):
                left[s] = left[s] - change[STRIP * s:STRIP * (s + 1), :BLK]
                right[s] = right[s] - change[STRIP * s:STRIP * (s + 1), BLK:]
    return jnp.concatenate(upper, axis=0), jnp.concatenate(inverse, axis=0)


def halves(x):
    high = x.astype(BF16)
    return high, (x - high.astype(F32)).astype(BF16)


def dot_nt3(lhs, rhs):
    def one(p, q):
        return lax.dot_general(p, q, (((1,), (1,)), ((), ())), preferred_element_type=F32)
    return one(lhs[0], rhs[0]) + (one(lhs[0], rhs[1]) + one(lhs[1], rhs[0]))


def dot_nn3(lhs, rhs):
    def one(p, q):
        return jnp.dot(p, q, preferred_element_type=F32)
    return one(lhs[0], rhs[0]) + (one(lhs[0], rhs[1]) + one(lhs[1], rhs[0]))


(SPREAD0, SPREAD1, SPREAD2, HEAD_A, HEAD_B, ACROSS_A, ACROSS_B, PAIR_A, PAIR_B, ROWS, ROWS_PAIR,
 ROWS_ON, SWAP, FIRST_Z, FIRST_Y, THEN_Y, THEN_Z, TILES) = range(18)
L_SLAB, L_OWN, L_HEAD, L_ROWS, L_SWAP, L_TILES, L_IN, L_OUT = 0, 1, 2, 3, 4, 5, 6, 8


def exchange_kernel(kr, tiles, panels, high, low, lower, slab, own, head, work, diag, whigh, wlow,
                    inbuf, hbuf, lbuf, ssem, rsem, lsem):
    g = lax.axis_index("row")
    c = lax.axis_index("col")
    core = lax.rem(c, 2)
    other = (c // 2) * 2 + 1 - core
    y, z = g // 4, lax.rem(g, 4)
    swap_row = (g // 8) * 8 + c
    swap_col = lax.rem(g, 8)
    is_self = swap_col == c
    mine = pl.multiple_of(c * 64, 64)
    not_self = jnp.logical_not(is_self)

    def send(src, dst, index, row, col):
        pltpu.make_async_remote_copy(
            src_ref=src, dst_ref=dst, send_sem=ssem.at[index], recv_sem=rsem.at[index],
            device_id=(row, col), device_id_type=MESH).start()

    def local(src, dst, index):
        pltpu.make_async_copy(src, dst, lsem.at[index]).start()

    def done(ref, sem):
        pltpu.make_async_copy(ref, ref, sem).wait()

    local(kr.at[:, :, pl.ds(0, 1024)], slab, L_SLAB)
    for a in range(2):
        for b in range(4):
            at = pl.multiple_of((b * 8 + c) * 512, 512)
            local(kr.at[a, :, pl.ds(at, 512)], own.at[a, b], L_OWN)

    barrier = pltpu.get_barrier_semaphore()

    @pl.loop(1, 16)
    def _(o):
        pl.semaphore_signal(barrier, inc=1, device_id=(lax.rem(g + o, 16), c), device_id_type=MESH)

    @pl.loop(1, 8)
    def _(o):
        pl.semaphore_signal(barrier, inc=1, device_id=(g, lax.rem(c + o, 8)), device_id_type=MESH)

    @pl.when(not_self)
    def _():
        pl.semaphore_signal(barrier, inc=1, device_id=(swap_row, swap_col), device_id_type=MESH)
        pl.semaphore_wait(barrier, 23)

    @pl.when(is_self)
    def _():
        pl.semaphore_wait(barrier, 22)

    done(slab, lsem.at[L_SLAB])

    def piece(which, q):
        return head.at[which, pl.ds(pl.multiple_of(mine + (q // 2) * 8, 8), 8),
                       pl.ds(pl.multiple_of(lax.rem(q, 2) * 256, 256), 256)]

    def spread(which, root, lanes_at, index):
        def src(q):
            return slab.at[0, pl.ds(pl.multiple_of((q // 2) * 8, 8), 8),
                           pl.ds(pl.multiple_of(lanes_at + lax.rem(q, 2) * 256, 256), 256)]

        @pl.when(g == root)
        def _():
            @pl.loop(1, 16)
            def _(o):
                q = lax.rem(g + o, 16)
                send(src(q), piece(which, q), index, q, c)
            local(src(g), piece(which, g), L_HEAD)

    spread(0, 0, 0, SPREAD0)
    spread(2, 1, 512, SPREAD2)
    spread(1, 0, 512, SPREAD1)

    def col_slab(a, r):
        return panels.at[2 + r // 8 + 2 * a, pl.ds(pl.multiple_of(lax.rem(r, 8) * 64, 64), 64), :]

    @pl.when(not_self)
    def _():
        for a in range(2):
            send(slab.at[a], col_slab(a, swap_row), SWAP, swap_row, swap_col)

    @pl.when(is_self)
    def _():
        for a in range(2):
            local(slab.at[a], col_slab(a, g), L_SWAP)

    def send_tiles(first, last):
        @pl.loop(1, 8)
        def _(o):
            cc = lax.rem(c + o, 8)
            for n in range(first, last):
                a, b = n // 4, n % 4
                at = pl.multiple_of((b * 8 + cc) * 512, 512)
                send(kr.at[a, :, pl.ds(at, 512)], tiles.at[a, b, pl.ds(mine, 64), :], TILES, g, cc)

    send_tiles(0, 1)

    def gather_head(which, index):
        @pl.loop(1, 16)
        def _(o):
            send(piece(which, g), piece(which, g), index, lax.rem(g + o, 16), c)

    def chunk(which, col):
        return head.at[which, pl.ds(pl.multiple_of(col * 64, 64), 64), :]

    def across(which, index):
        for o in range(1, 4):
            send(chunk(which, c), chunk(which, c), index, g, lax.rem(c + 2 * o, 8))

    def pair(which, index):
        for o in range(4):
            src = chunk(which, lax.rem(c + 2 * o, 8))
            send(src, src, index, g, other)

    @pl.when(g == 0)
    def _():
        done(head.at[0, pl.ds(0, 16), pl.ds(0, 256)], lsem.at[L_HEAD])

    @pl.when(g == 1)
    def _():
        done(head.at[0, pl.ds(0, 8), pl.ds(0, 256)], lsem.at[L_HEAD])

    @pl.when(g != 0)
    def _():
        done(piece(0, g), rsem.at[SPREAD0])

    gather_head(0, HEAD_A)

    @pl.when(g != 0)
    def _():
        done(piece(1, g), rsem.at[SPREAD1])

    @pl.when(g != 1)
    def _():
        done(piece(2, g), rsem.at[SPREAD2])

    gather_head(1, HEAD_B)
    gather_head(2, HEAD_B)
    done(head.at[0, pl.ds(0, 120), pl.ds(0, 256)], rsem.at[HEAD_A])
    across(0, ACROSS_A)
    done(head.at[1, pl.ds(0, 240), pl.ds(0, 256)], rsem.at[HEAD_B])
    across(1, ACROSS_B)
    across(2, ACROSS_B)

    for a in range(2):
        dst = panels.at[a, pl.ds(mine, 64), :]
        for o in range(1, 4):
            send(slab.at[a], dst, ROWS, g, lax.rem(c + 2 * o, 8))
        send(slab.at[a], dst, ROWS_PAIR, g, other)
        local(slab.at[a], dst, L_ROWS)

    send_tiles(1, 8)
    done(own, lsem.at[L_OWN])
    for a in range(2):
        for b in range(4):
            local(own.at[a, b], tiles.at[a, b, pl.ds(mine, 64), :], L_TILES)

    done(head.at[0, pl.ds(0, 192), :], rsem.at[ACROSS_A])
    pair(0, PAIR_A)

    @pl.when(not_self)
    def _():
        done(slab, rsem.at[SWAP])

    @pl.when(is_self)
    def _():
        done(slab, lsem.at[L_SWAP])

    def row_of(dy, dz):
        return lax.rem(y + dy, 4) * 4 + lax.rem(z + dz, 4)

    for o in range(1, 4):
        send(col_slab(0, g), col_slab(0, g), FIRST_Z, row_of(0, o), c)
        send(col_slab(1, g), col_slab(1, g), FIRST_Y, row_of(o, 0), c)

    def second_stage():
        three = panels.at[0, pl.ds(0, 192), :]
        done(three, rsem.at[FIRST_Z])
        done(three, rsem.at[FIRST_Y])

        @pl.loop(0, 4)
        def _(n):
            from_z, from_y = row_of(0, n), row_of(n, 0)
            for o in range(1, 4):
                send(col_slab(0, from_z), col_slab(0, from_z), THEN_Y, row_of(o, 0), c)
                send(col_slab(1, from_y), col_slab(1, from_y), THEN_Z, row_of(0, o), c)

    def rows_on():
        done(panels.at[0, pl.ds(0, 384), :], rsem.at[ROWS])
        for a in range(2):
            for o in range(1, 4):
                at = pl.multiple_of(lax.rem(c + 2 * o, 8) * 64, 64)
                src = panels.at[a, pl.ds(at, 64), :]
                send(src, src, ROWS_ON, g, other)

    done(head.at[0, pl.ds(0, 256), :], rsem.at[PAIR_A])

    lane_blk = lax.broadcasted_iota(jnp.int32, (BLK, 512), 1) // BLK
    blocks = 512 // BLK

    def factor(panel, between):
        @pl.loop(0, blocks)
        def _(kb):
            at = pl.multiple_of(kb * BLK, BLK)
            upper, inverse = factor_block(work[pl.ds(at, BLK), pl.ds(at, BLK)])
            diag[panel * blocks + kb] = upper
            strip = jnp.dot(inverse, work[pl.ds(at, BLK), :], precision=HI,
                            preferred_element_type=F32)
            work[pl.ds(at, BLK), :] = strip
            work[pl.ds(at, BLK), pl.ds(at, BLK)] = inverse

            @pl.loop(kb + 1, blocks)
            def _(rb):
                to = pl.multiple_of(rb * BLK, BLK)
                change = dot_tn(work[pl.ds(at, BLK), pl.ds(to, BLK)], work[pl.ds(at, BLK), :])
                old = work[pl.ds(to, BLK), :]
                work[pl.ds(to, BLK), :] = jnp.where(lane_blk == kb, F32(0.0), old) - change

            between(kb)

        for r in range(blocks):
            here = slice(r * BLK, (r + 1) * BLK)
            row = jnp.where(lane_blk <= r, work[here, :], F32(0.0))
            whigh[2 * panel, here, :], wlow[2 * panel, here, :] = halves(row)
            for s in range(blocks):
                there = slice(s * BLK, (s + 1) * BLK)
                if s > r:
                    lower[2 * panel, here, there] = jnp.zeros((BLK, BLK), F32)
                elif s == r:
                    lower[2 * panel, here, there] = diag[panel * blocks + r].T
                else:
                    lower[2 * panel, here, there] = work[there, here].T

    work[...] = head[0]

    def between(kb):
        @pl.when(kb == 0)
        def _():
            done(head.at[1, pl.ds(0, 384), :], rsem.at[ACROSS_B])
            pair(1, PAIR_B)
            pair(2, PAIR_B)

        @pl.when(kb == 1)
        def _():
            second_stage()

        @pl.when(kb == 3)
        def _():
            rows_on()

    factor(0, between)
    done(head.at[pl.ds(1, 2), pl.ds(0, 256), :], rsem.at[PAIR_B])

    right = dot_nn3((whigh[0], wlow[0]), halves(head[1]))
    whigh[1], wlow[1] = halves(right)
    lower[1] = right.T
    work[...] = head[2] - dot_tn(right, right)
    factor(1, lambda kb: None)

    done(panels.at[0, pl.ds(0, 128), :], rsem.at[ROWS_PAIR])
    done(panels.at[0, pl.ds(0, 384), :], rsem.at[ROWS_ON])
    done(slab, lsem.at[L_ROWS])
    twelve = panels.at[pl.ds(0, 2), pl.ds(0, 384), :]
    done(twelve, rsem.at[THEN_Y])
    done(twelve, rsem.at[THEN_Z])

    def fetch(t, slot):
        return pltpu.make_async_copy(panels.at[t], inbuf.at[slot], lsem.at[L_IN + slot])

    def store(t, slot):
        return (pltpu.make_async_copy(hbuf.at[slot], high.at[t], lsem.at[L_OUT + slot]),
                pltpu.make_async_copy(lbuf.at[slot], low.at[t], lsem.at[L_OUT + 2 + slot]))

    fetch(0, 0).start()

    @pl.loop(0, 6)
    def _(t):
        slot = lax.rem(t, 2)

        @pl.when(t < 5)
        def _():
            fetch(t + 1, 1 - slot).start()

        fetch(t, slot).wait()

        @pl.when(t >= 2)
        def _():
            for cp in store(t - 2, slot):
                cp.wait()

        first = dot_nt3(halves(inbuf[slot, :, :512]), (whigh[0], wlow[0]))
        top, rest = halves(first)
        hbuf[slot, :, :512], lbuf[slot, :, :512] = top, rest
        left = inbuf[slot, :, 512:] - dot_nn3((top, rest), (whigh[1], wlow[1]))
        hbuf[slot, :, 512:], lbuf[slot, :, 512:] = halves(
            dot_nt3(halves(left), (whigh[2], wlow[2])))
        for cp in store(t, slot):
            cp.start()

    for t in range(4, 6):
        for cp in store(t, t % 2):
            cp.wait()

    done(own, lsem.at[L_TILES])
    done(tiles.at[:, :, pl.ds(0, 448), :], rsem.at[TILES])
    done(tiles.at[:, :, pl.ds(0, 448), :], ssem.at[TILES])

    @pl.when(g == 0)
    def _():
        done(head.at[0, pl.ds(0, 120), pl.ds(0, 256)], ssem.at[SPREAD0])
        done(head.at[0, pl.ds(0, 120), pl.ds(0, 256)], ssem.at[SPREAD1])

    @pl.when(g == 1)
    def _():
        done(head.at[0, pl.ds(0, 120), pl.ds(0, 256)], ssem.at[SPREAD2])

    done(head.at[0, pl.ds(0, 120), pl.ds(0, 256)], ssem.at[HEAD_A])
    done(head.at[1, pl.ds(0, 240), pl.ds(0, 256)], ssem.at[HEAD_B])
    done(head.at[0, pl.ds(0, 192), :], ssem.at[ACROSS_A])
    done(head.at[1, pl.ds(0, 384), :], ssem.at[ACROSS_B])
    done(head.at[0, pl.ds(0, 256), :], ssem.at[PAIR_A])
    done(head.at[pl.ds(1, 2), pl.ds(0, 256), :], ssem.at[PAIR_B])
    done(panels.at[0, pl.ds(0, 384), :], ssem.at[ROWS])
    done(panels.at[0, pl.ds(0, 128), :], ssem.at[ROWS_PAIR])
    done(panels.at[0, pl.ds(0, 384), :], ssem.at[ROWS_ON])

    @pl.when(not_self)
    def _():
        done(slab, ssem.at[SWAP])

    three = panels.at[0, pl.ds(0, 192), :]
    done(three, ssem.at[FIRST_Z])
    done(three, ssem.at[FIRST_Y])
    done(twelve, ssem.at[THEN_Y])
    done(twelve, ssem.at[THEN_Z])


def exchange(rows):
    anyspace = pl.BlockSpec(memory_space=pl.ANY)
    return pl.pallas_call(
        exchange_kernel,
        out_shape=(
            jax.ShapeDtypeStruct((2, 4, 512, 512), F32),
            jax.ShapeDtypeStruct((6, 512, 1024), F32),
            jax.ShapeDtypeStruct((6, 512, 1024), BF16),
            jax.ShapeDtypeStruct((6, 512, 1024), BF16),
            jax.ShapeDtypeStruct((3, 512, 512), F32),
        ),
        in_specs=[anyspace],
        out_specs=(anyspace,) * 4 + (pl.BlockSpec(memory_space=pltpu.VMEM),),
        scratch_shapes=[
            pltpu.VMEM((2, 64, 1024), F32),
            pltpu.VMEM((2, 4, 64, 512), F32),
            pltpu.VMEM((3, 512, 512), F32),
            pltpu.VMEM((512, 512), F32),
            pltpu.VMEM((8, BLK, BLK), F32),
            pltpu.VMEM((3, 512, 512), BF16),
            pltpu.VMEM((3, 512, 512), BF16),
            pltpu.VMEM((2, 512, 1024), F32),
            pltpu.VMEM((2, 512, 1024), BF16),
            pltpu.VMEM((2, 512, 1024), BF16),
            pltpu.SemaphoreType.DMA((18,)),
            pltpu.SemaphoreType.DMA((18,)),
            pltpu.SemaphoreType.DMA((12,)),
        ],
        compiler_params=pltpu.CompilerParams(
            collective_id=1, has_side_effects=True, vmem_limit_bytes=48 * 1024 * 1024),
        name="exchange",
    )(rows)


def update_kernel(tiles, high_row, low_row, high_col, low_col, lower, out):
    g = lax.axis_index("row")
    c = lax.axis_index("col")
    a, half = pl.program_id(0), pl.program_id(1)
    flat = out.at[0].reshape(512 * 8, 128)
    left = (high_row[0], low_row[0])

    def put(slot, value):
        for n in range(4):
            flat[pl.ds(slot * 4 + n, 512, stride=8), :] = value[:, n * 128:(n + 1) * 128]

    for b in range(2):
        put(b, tiles[0, b] - dot_nt3(left, (high_col[b], low_col[b])))

    @pl.when((half == 0) & (c == 0))
    def _():
        put(0, high_row[0, :, :512].astype(F32) + low_row[0, :, :512].astype(F32))

    @pl.when((half == 0) & (c == 1))
    def _():
        put(0, high_row[0, :, 512:].astype(F32) + low_row[0, :, 512:].astype(F32))

    @pl.when((a == 0) & (g < 2))
    def _():
        flat[...] = jnp.zeros((512 * 8, 128), F32)

        @pl.when((half == 0) & (c <= g))
        def _():
            put(0, lower[g + c])


def update_tiles(tiles, high, low, lower):
    row_block = pl.BlockSpec((1, 512, 1024), lambda a, h: (a, 0, 0))
    col_block = pl.BlockSpec((2, 512, 1024), lambda a, h: (1 + h, 0, 0))
    return pl.pallas_call(
        update_kernel,
        grid=(2, 2),
        out_shape=jax.ShapeDtypeStruct((2, 512, 16, 128), F32),
        in_specs=[
            pl.BlockSpec((1, 2, 512, 512), lambda a, h: (a, h, 0, 0)),
            row_block, row_block, col_block, col_block,
            pl.BlockSpec((3, 512, 512), lambda a, h: (0, 0, 0)),
        ],
        out_specs=pl.BlockSpec((1, 512, 8, 128), lambda a, h: (a, 0, h, 0)),
        compiler_params=pltpu.CompilerParams(vmem_limit_bytes=56 * 1024 * 1024),
        name="update",
    )(tiles, high, low, high, low, lower)


def shards(kernel_rows):
    rows = kernel_rows.reshape(2, 64, 16384)
    tiles, panels, high, low, lower = exchange(rows)
    out = update_tiles(tiles, high, low, lower)
    return out.reshape(2, 1, 512, 4, 1, 512)


def solution(mesh):
    return jax.shard_map(
        shards,
        mesh=mesh,
        in_specs=(P(None, "row", "col", None, None),),
        out_specs=P(None, "row", None, None, "col", None),
        check_vma=False,
    )
```

time: 1110 us -> 205 us (0.18)
  the two profiles are of different devices: /device:TPU:1 before, /device:TPU:66 now
where the time goes in v2:
time: 205 us
  Pallas kernels  203 us (99%)
    pallas_call x1, Pallas kernels, exchange(): pl.pallas_call(exchange_kernel, out_shape=(jax.ShapeDtypeStruct((2, 4, 51...  182 us
    pallas_call x1, Pallas kernels, update_tiles(): pl.pallas_call(update_kernel, grid=(2, 2), out_shape=jax.ShapeDtypeStruct...  21.3 us

profile of v2, /device:TPU:66, one launch (start us, length us, event | category | flops | bytes accessed | tf_op | source)
XLA Modules:
  0.0 204.6 jit_solution(13797051548295290584)
XLA Ops:
  0.0 181.7 %exchange.1 = (f32[2,4,512,512]{3,2,1,0:T(8,128)}, f32[6,512,1024]{2,1,0:T(8,128)}, bf16[6,512,1024]{2,1,0:T(8,128)(2,1)}, bf16[6,512,1024]{2,1,0:T(8,128)(2,1)}, f32[3,512,512]{2,1,0:T(8,128)S(1)}) custom-call(f32[2,64,16384]{2,1,0:T(8,128)} %bitcast.2), custom_call_target="tpu_custom_call" | custom-call | tf_op jit(solution)/shard_map/exchange/pallas_call | solution.py:423
  181.7 0.0 copy-start
  181.7 1.6 copy-done
  183.3 21.3 %update.1 = f32[2,512,16,128]{3,2,1,0:T(8,128)} custom-call(f32[2,4,512,512]{3,2,1,0:T(8,128)} %get-tuple-element.9.tiles, bf16[6,512,1024]{2,1,0:T(8,128)(2,1)} %get-tuple-element.10.high_row.high_col, bf16[6,512,1024]{2,1,0:T(8,128)(2,1)} %get-tuple-element.11.low_row.low_col, bf16[6,512,1024]{2,1,0:T(8,128)(2,1)} %get-tuple-element.10.high_row.high_col, ...), custom_call_target="tpu_custom_call" | custom-call | tf_op jit(solution)/shard_map/update/pallas_call | solution.py:489
Async XLA Ops:
  181.7 1.7 copy-start

commit v3 on v2

--- a/solution.py
+++ b/solution.py
@@ -12,7 +12,6 @@
 BF16 = jnp.bfloat16
 BLK = 128
 STRIP = 8
-VMEM_CAP = 64 * 1024 * 1024 - 128 * 1024
 
 
 def dot_tn(lhs, rhs):
@@ -24,40 +23,58 @@
     count = BLK // STRIP
     lane = lax.broadcasted_iota(jnp.int32, (STRIP, BLK), 1)
     sublane = lax.broadcasted_iota(jnp.int32, (STRIP, BLK), 0)
-    left = [block[STRIP * t:STRIP * (t + 1), :] for t in range(count)]
-    right = [jnp.where(lane == sublane + STRIP * t, F32(1.0), F32(0.0)) for t in range(count)]
-    upper, inverse = [], []
+    zero, one = F32(0.0), F32(1.0)
+    span = range(STRIP)
+    strips = [block[STRIP * t:STRIP * (t + 1), :] for t in range(count)]
+    solved = []
+
+    def whole(strip, i):
+        return jnp.broadcast_to(strip[i:i + 1, :], (STRIP, BLK))
+
+    def single(strip, at):
+        return jnp.broadcast_to(strip[:, at:at + 1], (STRIP, BLK))
+
+    here_strip = strips[0]
+    cols = [single(here_strip, j) for j in span]
     for t in range(count):
-        row = [jnp.broadcast_to(left[t][i:i + 1, :], (STRIP, BLK)) for i in range(STRIP)]
-        inv = [jnp.broadcast_to(right[t][i:i + 1, :], (STRIP, BLK)) for i in range(STRIP)]
-        entry = {}
-        for i in range(STRIP):
-            for j in range(i, STRIP):
-                at = STRIP * t + j
-                entry[i, j] = jnp.broadcast_to(row[i][:, at:at + 1], (STRIP, BLK))
-        for k in range(STRIP):
-            scale = lax.rsqrt(entry[k, k])
-            row[k] = row[k] * scale
-            inv[k] = inv[k] * scale
-            factor = {i: entry[k, i] * scale for i in range(k + 1, STRIP)}
-            for i in range(k + 1, STRIP):
-                for j in range(i, STRIP):
-                    entry[i, j] = entry[i, j] - factor[i] * factor[j]
-                row[i] = row[i] - factor[i] * row[k]
-                inv[i] = inv[i] - factor[i] * inv[k]
-        strip_row, strip_inv = row[0], inv[0]
-        for i in range(1, STRIP):
-            strip_row = jnp.where(sublane == i, row[i], strip_row)
-            strip_inv = jnp.where(sublane == i, inv[i], strip_inv)
-        strip_row = jnp.where(lane >= sublane + STRIP * t, strip_row, F32(0.0))
-        upper.append(strip_row)
-        inverse.append(strip_inv)
-        if t + 1 < count:
-            change = dot_tn(strip_row, jnp.concatenate([strip_row, strip_inv], axis=1))
-            for s in range(t + 1, count):
-                left[s] = left[s] - change[STRIP * s:STRIP * (s + 1), :BLK]
-                right[s] = right[s] - change[STRIP * s:STRIP * (s + 1), BLK:]
-    return jnp.concatenate(upper, axis=0), jnp.concatenate(inverse, axis=0)
+        more = t + 1 < count
+        here = (lane >= STRIP * t) & (lane < STRIP * (t + 1))
+        here_strip = jnp.where(here, jnp.where(lane == STRIP * t + sublane, one, zero), here_strip)
+        if more:
+            pick = lane == STRIP * (t + 1) + sublane
+            next_strip = jnp.where(here, zero, strips[t + 1])
+            next_cols = [single(next_strip, STRIP * (t + 1) + j) for j in span]
+            sum_strip, sum_cols = None, [None] * STRIP
+        for k in span:
+            scale = lax.rsqrt(whole(cols[k], k))
+            factor = cols[k] * scale
+            for j in range(k + 1, STRIP):
+                cols[j] = cols[j] - factor * whole(factor, j)
+            row = whole(here_strip, k) * scale
+            below = jnp.where(sublane > k, factor, zero)
+            here_strip = jnp.where(sublane == k, row, here_strip - below * row)
+            if more:
+                across = jnp.sum(jnp.where(pick, row, zero), axis=1, keepdims=True)
+                across = jnp.broadcast_to(across, (STRIP, BLK))
+                terms = [across * row] + [across * whole(across, j) for j in span]
+                if k == 0:
+                    sum_strip, sum_cols = terms[0], terms[1:]
+                elif k < STRIP - 1:
+                    sum_strip = sum_strip + terms[0]
+                    sum_cols = [p + q for p, q in zip(sum_cols, terms[1:])]
+                else:
+                    next_strip = (next_strip - sum_strip) - terms[0]
+                    next_cols = [(b - p) - q for b, p, q in zip(next_cols, sum_cols, terms[1:])]
+        solved.append(here_strip)
+        if more:
+            last_strip = here_strip
+            here_strip, cols = next_strip, next_cols
+        if t + 2 < count:
+            change = dot_tn(last_strip, last_strip)
+            for s in range(t + 2, count):
+                strips[s] = jnp.where(here, zero, strips[s]) - change[STRIP * s:STRIP * (s + 1), :]
+    return jnp.concatenate(
+        [jnp.where(lane < STRIP * (t + 1), solved[t], zero) for t in range(count)], axis=0)
 
 
 def halves(x):
@@ -79,11 +96,12 @@
 
 (SPREAD0, SPREAD1, SPREAD2, HEAD_A, HEAD_B, ACROSS_A, ACROSS_B, PAIR_A, PAIR_B, ROWS, ROWS_PAIR,
  ROWS_ON, SWAP, FIRST_Z, FIRST_Y, THEN_Y, THEN_Z, TILES) = range(18)
-L_SLAB, L_OWN, L_HEAD, L_ROWS, L_SWAP, L_TILES, L_IN, L_OUT = 0, 1, 2, 3, 4, 5, 6, 8
-
-
-def exchange_kernel(kr, tiles, panels, high, low, lower, slab, own, head, work, diag, whigh, wlow,
-                    inbuf, hbuf, lbuf, ssem, rsem, lsem):
+SEMS = TILES + 8
+L_SLAB, L_OWN, L_HEAD, L_ROWS, L_SWAP, L_IN, L_OUT = 0, 1, 2, 3, 4, 5, 7
+
+
+def exchange_kernel(kr, out, panels, tiles, slab, head, work, diag, lower, whigh, wlow,
+                    inbuf, high, low, obuf, ssem, rsem, lsem):
     g = lax.axis_index("row")
     c = lax.axis_index("col")
     core = lax.rem(c, 2)
@@ -110,7 +128,7 @@
     for a in range(2):
         for b in range(4):
             at = pl.multiple_of((b * 8 + c) * 512, 512)
-            local(kr.at[a, :, pl.ds(at, 512)], own.at[a, b], L_OWN)
+            local(kr.at[a, :, pl.ds(at, 512)], tiles.at[a * 4 + b, pl.ds(mine, 64), :], L_OWN)
 
     barrier = pltpu.get_barrier_semaphore()
 
@@ -167,16 +185,15 @@
         for a in range(2):
             local(slab.at[a], col_slab(a, g), L_SWAP)
 
-    def send_tiles(first, last):
-        @pl.loop(1, 8)
-        def _(o):
-            cc = lax.rem(c + o, 8)
-            for n in range(first, last):
-                a, b = n // 4, n % 4
-                at = pl.multiple_of((b * 8 + cc) * 512, 512)
-                send(kr.at[a, :, pl.ds(at, 512)], tiles.at[a, b, pl.ds(mine, 64), :], TILES, g, cc)
-
-    send_tiles(0, 1)
+    def send_tiles():
+        @pl.loop(0, 8)
+        def _(n):
+            @pl.loop(1, 8)
+            def _(o):
+                cc = lax.rem(c + o, 8)
+                at = pl.multiple_of((lax.rem(n, 4) * 8 + cc) * 512, 512)
+                send(kr.at[n // 4, :, pl.ds(at, 512)], tiles.at[n, pl.ds(mine, 64), :],
+                     TILES + n, g, cc)
 
     def gather_head(which, index):
         @pl.loop(1, 16)
@@ -232,12 +249,7 @@
         send(slab.at[a], dst, ROWS_PAIR, g, other)
         local(slab.at[a], dst, L_ROWS)
 
-    send_tiles(1, 8)
-    done(own, lsem.at[L_OWN])
-    for a in range(2):
-        for b in range(4):
-            local(own.at[a, b], tiles.at[a, b, pl.ds(mine, 64), :], L_TILES)
-
+    send_tiles()
     done(head.at[0, pl.ds(0, 192), :], rsem.at[ACROSS_A])
     pair(0, PAIR_A)
 
@@ -280,16 +292,17 @@
 
     lane_blk = lax.broadcasted_iota(jnp.int32, (BLK, 512), 1) // BLK
     blocks = 512 // BLK
+    upper = (lax.broadcasted_iota(jnp.int32, (BLK, BLK), 0)
+             <= lax.broadcasted_iota(jnp.int32, (BLK, BLK), 1))
 
     def factor(panel, between):
         @pl.loop(0, blocks)
         def _(kb):
             at = pl.multiple_of(kb * BLK, BLK)
-            upper, inverse = factor_block(work[pl.ds(at, BLK), pl.ds(at, BLK)])
-            diag[panel * blocks + kb] = upper
-            strip = jnp.dot(inverse, work[pl.ds(at, BLK), :], precision=HI,
-                            preferred_element_type=F32)
-            work[pl.ds(at, BLK), :] = strip
+            inverse = factor_block(work[pl.ds(at, BLK), pl.ds(at, BLK)])
+            work[pl.ds(at, BLK), :] = jnp.dot(inverse, work[pl.ds(at, BLK), :], precision=HI,
+                                              preferred_element_type=F32)
+            diag[kb] = jnp.where(upper, work[pl.ds(at, BLK), pl.ds(at, BLK)], F32(0.0))
             work[pl.ds(at, BLK), pl.ds(at, BLK)] = inverse
 
             @pl.loop(kb + 1, blocks)
@@ -310,7 +323,7 @@
                 if s > r:
                     lower[2 * panel, here, there] = jnp.zeros((BLK, BLK), F32)
                 elif s == r:
-                    lower[2 * panel, here, there] = diag[panel * blocks + r].T
+                    lower[2 * panel, here, there] = diag[r].T
                 else:
                     lower[2 * panel, here, there] = work[there, here].T
 
@@ -344,15 +357,9 @@
     done(panels.at[0, pl.ds(0, 384), :], rsem.at[ROWS_ON])
     done(slab, lsem.at[L_ROWS])
     twelve = panels.at[pl.ds(0, 2), pl.ds(0, 384), :]
-    done(twelve, rsem.at[THEN_Y])
-    done(twelve, rsem.at[THEN_Z])
 
     def fetch(t, slot):
         return pltpu.make_async_copy(panels.at[t], inbuf.at[slot], lsem.at[L_IN + slot])
-
-    def store(t, slot):
-        return (pltpu.make_async_copy(hbuf.at[slot], high.at[t], lsem.at[L_OUT + slot]),
-                pltpu.make_async_copy(lbuf.at[slot], low.at[t], lsem.at[L_OUT + 2 + slot]))
 
     fetch(0, 0).start()
 
@@ -360,33 +367,80 @@
     def _(t):
         slot = lax.rem(t, 2)
 
+        @pl.when(t == 1)
+        def _():
+            done(twelve, rsem.at[THEN_Y])
+            done(twelve, rsem.at[THEN_Z])
+
         @pl.when(t < 5)
         def _():
             fetch(t + 1, 1 - slot).start()
 
         fetch(t, slot).wait()
-
-        @pl.when(t >= 2)
-        def _():
-            for cp in store(t - 2, slot):
-                cp.wait()
-
         first = dot_nt3(halves(inbuf[slot, :, :512]), (whigh[0], wlow[0]))
         top, rest = halves(first)
-        hbuf[slot, :, :512], lbuf[slot, :, :512] = top, rest
+        high[t, :, :512], low[t, :, :512] = top, rest
         left = inbuf[slot, :, 512:] - dot_nn3((top, rest), (whigh[1], wlow[1]))
-        hbuf[slot, :, 512:], lbuf[slot, :, 512:] = halves(
-            dot_nt3(halves(left), (whigh[2], wlow[2])))
-        for cp in store(t, slot):
-            cp.start()
-
-    for t in range(4, 6):
-        for cp in store(t, t % 2):
-            cp.wait()
-
-    done(own, lsem.at[L_TILES])
-    done(tiles.at[:, :, pl.ds(0, 448), :], rsem.at[TILES])
-    done(tiles.at[:, :, pl.ds(0, 448), :], ssem.at[TILES])
+        high[t, :, 512:], low[t, :, 512:] = halves(dot_nt3(halves(left), (whigh[2], wlow[2])))
+
+    done(tiles.at[0], lsem.at[L_OWN])
+
+    def leave(pair_no, slot):
+        at = pl.multiple_of(lax.rem(pair_no, 2) * 8, 8)
+        return pltpu.make_async_copy(
+            obuf.at[slot], out.at[pair_no // 2, :, pl.ds(at, 8), :], lsem.at[L_OUT + slot])
+
+    @pl.loop(0, 8)
+    def _(n):
+        a, b = n // 4, lax.rem(n, 4)
+        pair_no = n // 2
+        slot = lax.rem(pair_no, 2)
+        half = lax.rem(n, 2)
+        flat = obuf.at[slot].reshape(512 * 8, 128)
+
+        def put(value):
+            for m in range(4):
+                flat[pl.ds(half * 4 + m, 512, stride=8), :] = value[:, m * 128:(m + 1) * 128]
+
+        @pl.when((half == 0) & (pair_no >= 2))
+        def _():
+            leave(pair_no - 2, slot).wait()
+
+        done(tiles.at[n, pl.ds(0, 448), :], rsem.at[TILES + n])
+        special_row = (a == 0) & (g < 2)
+        special_col = (b == 0) & (c < 2)
+
+        @pl.when(jnp.logical_not(special_row | special_col))
+        def _():
+            put(tiles[n] - dot_nt3((high[a], low[a]), (high[2 + b], low[2 + b])))
+
+        @pl.when(special_col & jnp.logical_not(special_row) & (c == 0))
+        def _():
+            put(high[a, :, :512].astype(F32) + low[a, :, :512].astype(F32))
+
+        @pl.when(special_col & jnp.logical_not(special_row) & (c == 1))
+        def _():
+            put(high[a, :, 512:].astype(F32) + low[a, :, 512:].astype(F32))
+
+        for corner in range(3):
+            @pl.when(special_row & (b == 0) & (c <= g) & (g + c == corner))
+            def _():
+                put(lower[corner])
+
+        @pl.when(special_row & ((b > 0) | (c > g)))
+        def _():
+            put(jnp.zeros((512, 512), F32))
+
+        @pl.when(half == 1)
+        def _():
+            leave(pair_no, slot).start()
+
+    for pair_no in range(2, 4):
+        leave(pair_no, pair_no % 2).wait()
+
+    @pl.loop(0, 8)
+    def _(n):
+        done(tiles.at[n, pl.ds(0, 448), :], ssem.at[TILES + n])
 
     @pl.when(g == 0)
     def _():
@@ -423,88 +477,37 @@
     return pl.pallas_call(
         exchange_kernel,
         out_shape=(
-            jax.ShapeDtypeStruct((2, 4, 512, 512), F32),
+            jax.ShapeDtypeStruct((2, 512, 16, 128), F32),
             jax.ShapeDtypeStruct((6, 512, 1024), F32),
-            jax.ShapeDtypeStruct((6, 512, 1024), BF16),
-            jax.ShapeDtypeStruct((6, 512, 1024), BF16),
-            jax.ShapeDtypeStruct((3, 512, 512), F32),
         ),
         in_specs=[anyspace],
-        out_specs=(anyspace,) * 4 + (pl.BlockSpec(memory_space=pltpu.VMEM),),
+        out_specs=(anyspace,) * 2,
         scratch_shapes=[
+            pltpu.VMEM((8, 512, 512), F32),
             pltpu.VMEM((2, 64, 1024), F32),
-            pltpu.VMEM((2, 4, 64, 512), F32),
             pltpu.VMEM((3, 512, 512), F32),
             pltpu.VMEM((512, 512), F32),
-            pltpu.VMEM((8, BLK, BLK), F32),
+            pltpu.VMEM((4, BLK, BLK), F32),
+            pltpu.VMEM((3, 512, 512), F32),
             pltpu.VMEM((3, 512, 512), BF16),
             pltpu.VMEM((3, 512, 512), BF16),
             pltpu.VMEM((2, 512, 1024), F32),
-            pltpu.VMEM((2, 512, 1024), BF16),
-            pltpu.VMEM((2, 512, 1024), BF16),
-            pltpu.SemaphoreType.DMA((18,)),
-            pltpu.SemaphoreType.DMA((18,)),
-            pltpu.SemaphoreType.DMA((12,)),
+            pltpu.VMEM((6, 512, 1024), BF16),
+            pltpu.VMEM((6, 512, 1024), BF16),
+            pltpu.VMEM((2, 512, 8, 128), F32),
+            pltpu.SemaphoreType.DMA((SEMS,)),
+            pltpu.SemaphoreType.DMA((SEMS,)),
+            pltpu.SemaphoreType.DMA((9,)),
         ],
         compiler_params=pltpu.CompilerParams(
-            collective_id=1, has_side_effects=True, vmem_limit_bytes=48 * 1024 * 1024),
+            collective_id=1, has_side_effects=True, vmem_limit_bytes=56 * 1024 * 1024),
         name="exchange",
     )(rows)
 
 
-def update_kernel(tiles, high_row, low_row, high_col, low_col, lower, out):
-    g = lax.axis_index("row")
-    c = lax.axis_index("col")
-    a, half = pl.program_id(0), pl.program_id(1)
-    flat = out.at[0].reshape(512 * 8, 128)
-    left = (high_row[0], low_row[0])
-
-    def put(slot, value):
-        for n in range(4):
-            flat[pl.ds(slot * 4 + n, 512, stride=8), :] = value[:, n * 128:(n + 1) * 128]
-
-    for b in range(2):
-        put(b, tiles[0, b] - dot_nt3(left, (high_col[b], low_col[b])))
-
-    @pl.when((half == 0) & (c == 0))
-    def _():
-        put(0, high_row[0, :, :512].astype(F32) + low_row[0, :, :512].astype(F32))
-
-    @pl.when((half == 0) & (c == 1))
-    def _():
-        put(0, high_row[0, :, 512:].astype(F32) + low_row[0, :, 512:].astype(F32))
-
-    @pl.when((a == 0) & (g < 2))
-    def _():
-        flat[...] = jnp.zeros((512 * 8, 128), F32)
-
-        @pl.when((half == 0) & (c <= g))
-        def _():
-            put(0, lower[g + c])
-
-
-def update_tiles(tiles, high, low, lower):
-    row_block = pl.BlockSpec((1, 512, 1024), lambda a, h: (a, 0, 0))
-    col_block = pl.BlockSpec((2, 512, 1024), lambda a, h: (1 + h, 0, 0))
-    return pl.pallas_call(
-        update_kernel,
-        grid=(2, 2),
-        out_shape=jax.ShapeDtypeStruct((2, 512, 16, 128), F32),
-        in_specs=[
-            pl.BlockSpec((1, 2, 512, 512), lambda a, h: (a, h, 0, 0)),
-            row_block, row_block, col_block, col_block,
-            pl.BlockSpec((3, 512, 512), lambda a, h: (0, 0, 0)),
-        ],
-        out_specs=pl.BlockSpec((1, 512, 8, 128), lambda a, h: (a, 0, h, 0)),
-        compiler_params=pltpu.CompilerParams(vmem_limit_bytes=56 * 1024 * 1024),
-        name="update",
-    )(tiles, high, low, high, low, lower)
-
-
 def shards(kernel_rows):
     rows = kernel_rows.reshape(2, 64, 16384)
-    tiles, panels, high, low, lower = exchange(rows)
-    out = update_tiles(tiles, high, low, lower)
+    out, _ = exchange(rows)
     return out.reshape(2, 1, 512, 4, 1, 512)
 
 

time: 205 us -> 178 us (0.87)
  the two profiles are of different devices: /device:TPU:66 before, /device:TPU:1 now
where the time goes in v3:
time: 178 us
  Pallas kernels  170 us (96%)
  local copies, waits for them, and re-layouts  8.03 us (5%)
    pallas_call x1, Pallas kernels, exchange(): pl.pallas_call(exchange_kernel, out_shape=(jax.ShapeDtypeStruct((2, 512,...  170 us
    unnamed x1, local copies, waits for them, and re-layouts  8.03 us

profile of v3, /device:TPU:1, one launch (start us, length us, event | category | flops | bytes accessed | tf_op | source)
XLA Modules:
  0.0 178.1 jit_solution(14749661794800309633)
XLA Ops:
  0.0 170.1 %exchange.1 = (f32[2,512,16,128]{3,2,1,0:T(8,128)}, f32[6,512,1024]{2,1,0:T(8,128)}) custom-call(f32[2,64,16384]{2,1,0:T(8,128)} %bitcast.2), custom_call_target="tpu_custom_call" | custom-call | tf_op jit(solution)/shard_map/exchange/pallas_call | solution.py:477
  170.1 8.0 %copy.4 = f32[2,1,512,4,1,512]{5,4,3,2,1,0:T(1,128)} copy(f32[2,1,512,4,1,512]{5,4,3,2,1,0:T(1,128)} %bitcast.3) | data formatting | bytes 16777216

commit v4 on v3

--- a/solution.py
+++ b/solution.py
@@ -96,12 +96,13 @@
 
 (SPREAD0, SPREAD1, SPREAD2, HEAD_A, HEAD_B, ACROSS_A, ACROSS_B, PAIR_A, PAIR_B, ROWS, ROWS_PAIR,
  ROWS_ON, SWAP, FIRST_Z, FIRST_Y, THEN_Y, THEN_Z, TILES) = range(18)
-SEMS = TILES + 8
-L_SLAB, L_OWN, L_HEAD, L_ROWS, L_SWAP, L_IN, L_OUT = 0, 1, 2, 3, 4, 5, 7
+TURNED = TILES + 8
+SEMS = TURNED + 4
+L_SLAB, L_OWN, L_HEAD, L_ROWS, L_SWAP, L_IN, L_OUT, L_TURNED = 0, 1, 2, 3, 4, 5, 7, 9
 
 
 def exchange_kernel(kr, out, panels, tiles, slab, head, work, diag, lower, whigh, wlow,
-                    inbuf, high, low, obuf, ssem, rsem, lsem):
+                    inbuf, high, low, obuf, turned, ssem, rsem, lsem):
     g = lax.axis_index("row")
     c = lax.axis_index("col")
     core = lax.rem(c, 2)
@@ -112,6 +113,9 @@
     is_self = swap_col == c
     mine = pl.multiple_of(c * 64, 64)
     not_self = jnp.logical_not(is_self)
+    chip = c // 2
+    ahead = lax.rem(chip - swap_col // 2 + 4, 4)
+    gives = ahead != 2
 
     def send(src, dst, index, row, col):
         pltpu.make_async_remote_copy(
@@ -143,11 +147,17 @@
     @pl.when(not_self)
     def _():
         pl.semaphore_signal(barrier, inc=1, device_id=(swap_row, swap_col), device_id_type=MESH)
-        pl.semaphore_wait(barrier, 23)
-
-    @pl.when(is_self)
-    def _():
-        pl.semaphore_wait(barrier, 22)
+
+    for half in range(2):
+        for o in range(-2, 4):
+            src_row, src_col = c + 8 * half, lax.rem((c // 2) * 2 + o + 8, 8)
+
+            @pl.when((src_row != g) | (src_col != c))
+            def _():
+                pl.semaphore_signal(barrier, inc=1, device_id=(src_row, src_col),
+                                    device_id_type=MESH)
+
+    pl.semaphore_wait(barrier, 22 + jnp.where(is_self, 15, 1 + jnp.where(gives, 16, 0)))
 
     done(slab, lsem.at[L_SLAB])
 
@@ -185,8 +195,8 @@
         for a in range(2):
             local(slab.at[a], col_slab(a, g), L_SWAP)
 
-    def send_tiles():
-        @pl.loop(0, 8)
+    def send_tiles(first, last):
+        @pl.loop(first, last)
         def _(n):
             @pl.loop(1, 8)
             def _(o):
@@ -195,6 +205,60 @@
                 send(kr.at[n // 4, :, pl.ds(at, 512)], tiles.at[n, pl.ds(mine, 64), :],
                      TILES + n, g, cc)
 
+    def lanes(group):
+        return pl.ds(pl.multiple_of(group * BLK, BLK), BLK)
+
+    def send_parts():
+        @pl.loop(4, 8)
+        def _(n):
+            def part(cc, group):
+                at = pl.multiple_of(((n - 4) * 8 + cc) * 512 + group * BLK, BLK)
+                send(kr.at[1, :, pl.ds(at, BLK)], tiles.at[n, pl.ds(mine, 64), lanes(group)],
+                     TILES + n, g, cc)
+
+            at = pl.multiple_of(((n - 4) * 8 + other) * 512, 512)
+            send(kr.at[1, :, pl.ds(at, 512)], tiles.at[n, pl.ds(mine, 64), :], TILES + n, g, other)
+            for o in (1, 2, 3):
+                there = lax.rem(chip + o, 4)
+                for k in range(2):
+                    if o == 2:
+                        part(there * 2 + k, chip)
+                    else:
+                        for q in range(1, 4):
+                            part(there * 2 + k, lax.rem(there + q, 4))
+
+    def send_turned():
+        home = swap_col // 2
+        rows = pl.ds(pl.multiple_of(core * 64, 64), 64)
+
+        def block(a, to, group):
+            at = pl.multiple_of((16 + to) * 512 + group * BLK, BLK)
+            return kr.at[a, :, pl.ds(at, BLK)]
+
+        @pl.loop(0, 16)
+        def _(o):
+            to = lax.rem(g + o, 16)
+            away = (to != g) | not_self
+            for a in range(2):
+                b = g // 8 + 2 * a
+                for q in range(1, 4):
+                    @pl.when((ahead == 0) & away)
+                    def _():
+                        send(block(a, to, lax.rem(home + q, 4)), turned.at[b, q - 1, rows, :],
+                             TURNED + b, to, swap_col)
+
+                    @pl.when((ahead == 0) & jnp.logical_not(away))
+                    def _():
+                        local(block(a, to, lax.rem(home + q, 4)), turned.at[b, q - 1, rows, :],
+                              L_TURNED)
+                for d, slot in ((1, 3), (3, 4)):
+                    @pl.when(ahead == d)
+                    def _():
+                        send(block(a, to, lax.rem(home + 2, 4)), turned.at[b, slot, rows, :],
+                             TURNED + b, to, swap_col)
+
+    send_tiles(0, 1)
+
     def gather_head(which, index):
         @pl.loop(1, 16)
         def _(o):
@@ -238,6 +302,22 @@
     gather_head(2, HEAD_B)
     done(head.at[0, pl.ds(0, 120), pl.ds(0, 256)], rsem.at[HEAD_A])
     across(0, ACROSS_A)
+
+    @pl.when(not_self)
+    def _():
+        done(slab, rsem.at[SWAP])
+
+    @pl.when(is_self)
+    def _():
+        done(slab, lsem.at[L_SWAP])
+
+    def row_of(dy, dz):
+        return lax.rem(y + dy, 4) * 4 + lax.rem(z + dz, 4)
+
+    for o in range(1, 4):
+        send(col_slab(0, g), col_slab(0, g), FIRST_Z, row_of(0, o), c)
+        send(col_slab(1, g), col_slab(1, g), FIRST_Y, row_of(o, 0), c)
+
     done(head.at[1, pl.ds(0, 240), pl.ds(0, 256)], rsem.at[HEAD_B])
     across(1, ACROSS_B)
     across(2, ACROSS_B)
@@ -249,24 +329,10 @@
         send(slab.at[a], dst, ROWS_PAIR, g, other)
         local(slab.at[a], dst, L_ROWS)
 
-    send_tiles()
+    send_tiles(1, 4)
+    send_parts()
     done(head.at[0, pl.ds(0, 192), :], rsem.at[ACROSS_A])
     pair(0, PAIR_A)
-
-    @pl.when(not_self)
-    def _():
-        done(slab, rsem.at[SWAP])
-
-    @pl.when(is_self)
-    def _():
-        done(slab, lsem.at[L_SWAP])
-
-    def row_of(dy, dz):
-        return lax.rem(y + dy, 4) * 4 + lax.rem(z + dz, 4)
-
-    for o in range(1, 4):
-        send(col_slab(0, g), col_slab(0, g), FIRST_Z, row_of(0, o), c)
-        send(col_slab(1, g), col_slab(1, g), FIRST_Y, row_of(o, 0), c)
 
     def second_stage():
         three = panels.at[0, pl.ds(0, 192), :]
@@ -332,13 +398,17 @@
     def between(kb):
         @pl.when(kb == 0)
         def _():
+            second_stage()
+
+        @pl.when(kb == 1)
+        def _():
             done(head.at[1, pl.ds(0, 384), :], rsem.at[ACROSS_B])
             pair(1, PAIR_B)
             pair(2, PAIR_B)
 
-        @pl.when(kb == 1)
-        def _():
-            second_stage()
+        @pl.when(kb == 2)
+        def _():
+            send_turned()
 
         @pl.when(kb == 3)
         def _():
@@ -384,6 +454,27 @@
         high[t, :, 512:], low[t, :, 512:] = halves(dot_nt3(halves(left), (whigh[2], wlow[2])))
 
     done(tiles.at[0], lsem.at[L_OWN])
+
+    @pl.when(is_self)
+    def _():
+        done(tiles.at[0, pl.ds(0, 96), :], lsem.at[L_TURNED])
+
+    def turn(n):
+        b = n - 4
+        own_source = is_self & (lax.rem(b, 2) == g // 8)
+
+        @pl.when(own_source)
+        def _():
+            done(tiles.at[0, pl.ds(0, 112), :], rsem.at[TURNED + b])
+
+        @pl.when(jnp.logical_not(own_source))
+        def _():
+            done(turned.at[b], rsem.at[TURNED + b])
+
+        places = ((1, 0), (2, 0), (3, 0), (2, 1), (2, 3))
+        for slot, (down, right) in enumerate(places):
+            tiles[n, lanes(lax.rem(chip + down, 4)), lanes(lax.rem(chip + right, 4))] = (
+                turned[b, slot].T)
 
     def leave(pair_no, slot):
         at = pl.multiple_of(lax.rem(pair_no, 2) * 8, 8)
@@ -406,7 +497,15 @@
         def _():
             leave(pair_no - 2, slot).wait()
 
-        done(tiles.at[n, pl.ds(0, 448), :], rsem.at[TILES + n])
+        @pl.when(n < 4)
+        def _():
+            done(tiles.at[n, pl.ds(0, 448), :], rsem.at[TILES + n])
+
+        @pl.when(n >= 4)
+        def _():
+            done(tiles.at[n, pl.ds(0, 288), :], rsem.at[TILES + n])
+            turn(n)
+
         special_row = (a == 0) & (g < 2)
         special_col = (b == 0) & (c < 2)
 
@@ -438,9 +537,25 @@
     for pair_no in range(2, 4):
         leave(pair_no, pair_no % 2).wait()
 
-    @pl.loop(0, 8)
+    @pl.loop(0, 4)
     def _(n):
         done(tiles.at[n, pl.ds(0, 448), :], ssem.at[TILES + n])
+        done(tiles.at[n, pl.ds(0, 288), :], ssem.at[TILES + 4 + n])
+
+    for a in range(2):
+        index = TURNED + g // 8 + 2 * a
+
+        @pl.when((ahead == 0) & not_self)
+        def _():
+            done(tiles.at[pl.ds(0, 3), pl.ds(0, 256), :], ssem.at[index])
+
+        @pl.when(is_self)
+        def _():
+            done(tiles.at[pl.ds(0, 3), pl.ds(0, 240), :], ssem.at[index])
+
+        @pl.when((ahead == 1) | (ahead == 3))
+        def _():
+            done(tiles.at[0, pl.ds(0, 256), :], ssem.at[index])
 
     @pl.when(g == 0)
     def _():
@@ -495,9 +610,10 @@
             pltpu.VMEM((6, 512, 1024), BF16),
             pltpu.VMEM((6, 512, 1024), BF16),
             pltpu.VMEM((2, 512, 8, 128), F32),
+            pltpu.VMEM((4, 5, BLK, BLK), F32),
             pltpu.SemaphoreType.DMA((SEMS,)),
             pltpu.SemaphoreType.DMA((SEMS,)),
-            pltpu.SemaphoreType.DMA((9,)),
+            pltpu.SemaphoreType.DMA((10,)),
         ],
         compiler_params=pltpu.CompilerParams(
             collective_id=1, has_side_effects=True, vmem_limit_bytes=56 * 1024 * 1024),

time: 178 us -> 195 us (1.096)
  the two profiles are of different devices: /device:TPU:1 before, /device:TPU:114 now
where the time goes in v4:
time: 195 us
  Pallas kernels  187 us (96%)
  local copies, waits for them, and re-layouts  8.03 us (4%)
    pallas_call x1, Pallas kernels, exchange(): pl.pallas_call(exchange_kernel, out_shape=(jax.ShapeDtypeStruct((2, 512,...  187 us
    unnamed x1, local copies, waits for them, and re-layouts  8.03 us

profile of v4, /device:TPU:114, one launch (start us, length us, event | category | flops | bytes accessed | tf_op | source)
XLA Modules:
  0.0 195.4 jit_solution(14997363673062453601)
XLA Ops:
  0.0 187.4 %exchange.1 = (f32[2,512,16,128]{3,2,1,0:T(8,128)}, f32[6,512,1024]{2,1,0:T(8,128)}) custom-call(f32[2,64,16384]{2,1,0:T(8,128)} %bitcast.2), custom_call_target="tpu_custom_call" | custom-call | tf_op jit(solution)/shard_map/exchange/pallas_call | solution.py:592
  187.4 8.0 %copy.4 = f32[2,1,512,4,1,512]{5,4,3,2,1,0:T(1,128)} copy(f32[2,1,512,4,1,512]{5,4,3,2,1,0:T(1,128)} %bitcast.3) | data formatting | bytes 16777216

commit v5 on v3

--- a/solution.py
+++ b/solution.py
@@ -96,12 +96,13 @@
 
 (SPREAD0, SPREAD1, SPREAD2, HEAD_A, HEAD_B, ACROSS_A, ACROSS_B, PAIR_A, PAIR_B, ROWS, ROWS_PAIR,
  ROWS_ON, SWAP, FIRST_Z, FIRST_Y, THEN_Y, THEN_Z, TILES) = range(18)
-SEMS = TILES + 8
-L_SLAB, L_OWN, L_HEAD, L_ROWS, L_SWAP, L_IN, L_OUT = 0, 1, 2, 3, 4, 5, 7
+TURNED = TILES + 8
+SEMS = TURNED + 8
+L_SLAB, L_OWN, L_HEAD, L_ROWS, L_SWAP, L_IN, L_OUT, L_TURNED = 0, 1, 2, 3, 4, 5, 7, 9
 
 
 def exchange_kernel(kr, out, panels, tiles, slab, head, work, diag, lower, whigh, wlow,
-                    inbuf, high, low, obuf, ssem, rsem, lsem):
+                    inbuf, high, low, obuf, turned, ssem, rsem, lsem):
     g = lax.axis_index("row")
     c = lax.axis_index("col")
     core = lax.rem(c, 2)
@@ -112,6 +113,8 @@
     is_self = swap_col == c
     mine = pl.multiple_of(c * 64, 64)
     not_self = jnp.logical_not(is_self)
+    chip = c // 2
+    gives = chip == swap_col // 2
 
     def send(src, dst, index, row, col):
         pltpu.make_async_remote_copy(
@@ -143,11 +146,17 @@
     @pl.when(not_self)
     def _():
         pl.semaphore_signal(barrier, inc=1, device_id=(swap_row, swap_col), device_id_type=MESH)
-        pl.semaphore_wait(barrier, 23)
-
-    @pl.when(is_self)
-    def _():
-        pl.semaphore_wait(barrier, 22)
+
+    for half in range(2):
+        for o in range(2):
+            src_row, src_col = c + 8 * half, chip * 2 + o
+
+            @pl.when((src_row != g) | (src_col != c))
+            def _():
+                pl.semaphore_signal(barrier, inc=1, device_id=(src_row, src_col),
+                                    device_id_type=MESH)
+
+    pl.semaphore_wait(barrier, 22 + jnp.where(is_self, 15, 1 + jnp.where(gives, 16, 0)))
 
     done(slab, lsem.at[L_SLAB])
 
@@ -185,15 +194,57 @@
         for a in range(2):
             local(slab.at[a], col_slab(a, g), L_SWAP)
 
-    def send_tiles():
-        @pl.loop(0, 8)
+    def lanes(group):
+        return pl.ds(pl.multiple_of(group * BLK, BLK), BLK)
+
+    def send_parts(first, last):
+        @pl.loop(first, last)
         def _(n):
-            @pl.loop(1, 8)
+            a, b = n // 4, lax.rem(n, 4)
+
+            def whole(cc):
+                at = pl.multiple_of((b * 8 + cc) * 512, 512)
+                send(kr.at[a, :, pl.ds(at, 512)], tiles.at[n, pl.ds(mine, 64), :],
+                     TILES + n, g, cc)
+
+            whole(other)
+            for k in range(2):
+                whole(lax.rem(chip + 1, 4) * 2 + k)
+                whole(lax.rem(chip + 3, 4) * 2 + k)
+            there = lax.rem(chip + 2, 4)
+            for k in range(2):
+                for q in range(1, 4):
+                    group = lax.rem(there + q, 4)
+                    at = pl.multiple_of((b * 8 + there * 2 + k) * 512 + group * BLK, BLK)
+                    send(kr.at[a, :, pl.ds(at, BLK)], tiles.at[n, pl.ds(mine, 64), lanes(group)],
+                         TILES + n, g, there * 2 + k)
+
+    def send_turned(first, last):
+        far = lax.rem(swap_col // 2 + 2, 4)
+        rows = pl.ds(pl.multiple_of(core * 64, 64), 64)
+
+        @pl.when(gives)
+        def _():
+            @pl.loop(0, 16)
             def _(o):
-                cc = lax.rem(c + o, 8)
-                at = pl.multiple_of((lax.rem(n, 4) * 8 + cc) * 512, 512)
-                send(kr.at[n // 4, :, pl.ds(at, 512)], tiles.at[n, pl.ds(mine, 64), :],
-                     TILES + n, g, cc)
+                to = lax.rem(g + o, 16)
+                away = (to != g) | not_self
+                for dest_a in range(first, last):
+                    for a in range(2):
+                        n = dest_a * 4 + g // 8 + 2 * a
+                        at = pl.multiple_of((dest_a * 16 + to) * 512 + far * BLK, BLK)
+                        src = kr.at[a, :, pl.ds(at, BLK)]
+                        dst = turned.at[n, rows, :]
+
+                        @pl.when(away)
+                        def _():
+                            send(src, dst, TURNED + n, to, swap_col)
+
+                        @pl.when(jnp.logical_not(away))
+                        def _():
+                            local(src, dst, L_TURNED)
+
+    send_parts(0, 1)
 
     def gather_head(which, index):
         @pl.loop(1, 16)
@@ -238,6 +289,22 @@
     gather_head(2, HEAD_B)
     done(head.at[0, pl.ds(0, 120), pl.ds(0, 256)], rsem.at[HEAD_A])
     across(0, ACROSS_A)
+
+    @pl.when(not_self)
+    def _():
+        done(slab, rsem.at[SWAP])
+
+    @pl.when(is_self)
+    def _():
+        done(slab, lsem.at[L_SWAP])
+
+    def row_of(dy, dz):
+        return lax.rem(y + dy, 4) * 4 + lax.rem(z + dz, 4)
+
+    for o in range(1, 4):
+        send(col_slab(0, g), col_slab(0, g), FIRST_Z, row_of(0, o), c)
+        send(col_slab(1, g), col_slab(1, g), FIRST_Y, row_of(o, 0), c)
+
     done(head.at[1, pl.ds(0, 240), pl.ds(0, 256)], rsem.at[HEAD_B])
     across(1, ACROSS_B)
     across(2, ACROSS_B)
@@ -249,24 +316,9 @@
         send(slab.at[a], dst, ROWS_PAIR, g, other)
         local(slab.at[a], dst, L_ROWS)
 
-    send_tiles()
+    send_parts(1, 8)
     done(head.at[0, pl.ds(0, 192), :], rsem.at[ACROSS_A])
     pair(0, PAIR_A)
-
-    @pl.when(not_self)
-    def _():
-        done(slab, rsem.at[SWAP])
-
-    @pl.when(is_self)
-    def _():
-        done(slab, lsem.at[L_SWAP])
-
-    def row_of(dy, dz):
-        return lax.rem(y + dy, 4) * 4 + lax.rem(z + dz, 4)
-
-    for o in range(1, 4):
-        send(col_slab(0, g), col_slab(0, g), FIRST_Z, row_of(0, o), c)
-        send(col_slab(1, g), col_slab(1, g), FIRST_Y, row_of(o, 0), c)
 
     def second_stage():
         three = panels.at[0, pl.ds(0, 192), :]
@@ -332,13 +384,17 @@
     def between(kb):
         @pl.when(kb == 0)
         def _():
+            second_stage()
+
+        @pl.when(kb == 1)
+        def _():
             done(head.at[1, pl.ds(0, 384), :], rsem.at[ACROSS_B])
             pair(1, PAIR_B)
             pair(2, PAIR_B)
 
-        @pl.when(kb == 1)
-        def _():
-            second_stage()
+        @pl.when(kb == 2)
+        def _():
+            send_turned(0, 2)
 
         @pl.when(kb == 3)
         def _():
@@ -384,6 +440,23 @@
         high[t, :, 512:], low[t, :, 512:] = halves(dot_nt3(halves(left), (whigh[2], wlow[2])))
 
     done(tiles.at[0], lsem.at[L_OWN])
+
+    @pl.when(is_self)
+    def _():
+        done(tiles.at[0, pl.ds(0, 64), :], lsem.at[L_TURNED])
+
+    def turn(n):
+        own_source = is_self & (lax.rem(n, 2) == g // 8)
+
+        @pl.when(own_source)
+        def _():
+            done(tiles.at[0, pl.ds(0, 16), :], rsem.at[TURNED + n])
+
+        @pl.when(jnp.logical_not(own_source))
+        def _():
+            done(turned.at[n], rsem.at[TURNED + n])
+
+        tiles[n, lanes(lax.rem(chip + 2, 4)), lanes(chip)] = turned[n].T
 
     def leave(pair_no, slot):
         at = pl.multiple_of(lax.rem(pair_no, 2) * 8, 8)
@@ -406,7 +479,8 @@
         def _():
             leave(pair_no - 2, slot).wait()
 
-        done(tiles.at[n, pl.ds(0, 448), :], rsem.at[TILES + n])
+        done(tiles.at[n, pl.ds(0, 416), :], rsem.at[TILES + n])
+        turn(n)
         special_row = (a == 0) & (g < 2)
         special_col = (b == 0) & (c < 2)
 
@@ -440,7 +514,19 @@
 
     @pl.loop(0, 8)
     def _(n):
-        done(tiles.at[n, pl.ds(0, 448), :], ssem.at[TILES + n])
+        done(tiles.at[n, pl.ds(0, 416), :], ssem.at[TILES + n])
+
+    for dest_a in range(0, 2):
+        for a in range(2):
+            index = TURNED + dest_a * 4 + g // 8 + 2 * a
+
+            @pl.when(gives & not_self)
+            def _():
+                done(tiles.at[0, pl.ds(0, 256), :], ssem.at[index])
+
+            @pl.when(is_self)
+            def _():
+                done(tiles.at[0, pl.ds(0, 240), :], ssem.at[index])
 
     @pl.when(g == 0)
     def _():
@@ -495,9 +581,10 @@
             pltpu.VMEM((6, 512, 1024), BF16),
             pltpu.VMEM((6, 512, 1024), BF16),
             pltpu.VMEM((2, 512, 8, 128), F32),
+            pltpu.VMEM((8, BLK, BLK), F32),
             pltpu.SemaphoreType.DMA((SEMS,)),
             pltpu.SemaphoreType.DMA((SEMS,)),
-            pltpu.SemaphoreType.DMA((9,)),
+            pltpu.SemaphoreType.DMA((10,)),
         ],
         compiler_params=pltpu.CompilerParams(
             collective_id=1, has_side_effects=True, vmem_limit_bytes=56 * 1024 * 1024),

time: 178 us -> 164 us (0.921)
  Pallas kernels: 170 us -> 156 us
    pallas_call x1, Pallas kernels: 170 us -> 156 us  [exchange(): pl.pallas_call(exchange_kernel, out_shape=(jax.ShapeDtypeStruct((2, 512,...]
where the time goes in v5:
time: 164 us
  Pallas kernels  156 us (95%)
  local copies, waits for them, and re-layouts  8.03 us (5%)
    pallas_call x1, Pallas kernels, exchange(): pl.pallas_call(exchange_kernel, out_shape=(jax.ShapeDtypeStruct((2, 512,...  156 us
    unnamed x1, local copies, waits for them, and re-layouts  8.03 us

profile of v5, /device:TPU:1, one launch (start us, length us, event | category | flops | bytes accessed | tf_op | source)
XLA Modules:
  0.0 163.7 jit_solution(16255544272729771830)
XLA Ops:
  0.0 155.7 %exchange.1 = (f32[2,512,16,128]{3,2,1,0:T(8,128)}, f32[6,512,1024]{2,1,0:T(8,128)}) custom-call(f32[2,64,16384]{2,1,0:T(8,128)} %bitcast.2), custom_call_target="tpu_custom_call" | custom-call | tf_op jit(solution)/shard_map/exchange/pallas_call | solution.py:563
  155.7 8.0 %copy.4 = f32[2,1,512,4,1,512]{5,4,3,2,1,0:T(1,128)} copy(f32[2,1,512,4,1,512]{5,4,3,2,1,0:T(1,128)} %bitcast.3) | data formatting | bytes 16777216

commit v6 on v5

--- a/solution.py
+++ b/solution.py
@@ -97,7 +97,9 @@
 (SPREAD0, SPREAD1, SPREAD2, HEAD_A, HEAD_B, ACROSS_A, ACROSS_B, PAIR_A, PAIR_B, ROWS, ROWS_PAIR,
  ROWS_ON, SWAP, FIRST_Z, FIRST_Y, THEN_Y, THEN_Z, TILES) = range(18)
 TURNED = TILES + 8
-SEMS = TURNED + 8
+ROWS_FAR = TURNED + 8
+ROWS_FAR_ON = ROWS_FAR + 1
+SEMS = ROWS_FAR + 2
 L_SLAB, L_OWN, L_HEAD, L_ROWS, L_SWAP, L_IN, L_OUT, L_TURNED = 0, 1, 2, 3, 4, 5, 7, 9
 
 
@@ -311,12 +313,12 @@
 
     for a in range(2):
         dst = panels.at[a, pl.ds(mine, 64), :]
-        for o in range(1, 4):
+        for o in (1, 3):
             send(slab.at[a], dst, ROWS, g, lax.rem(c + 2 * o, 8))
         send(slab.at[a], dst, ROWS_PAIR, g, other)
         local(slab.at[a], dst, L_ROWS)
 
-    send_parts(1, 8)
+    send_parts(1, 4)
     done(head.at[0, pl.ds(0, 192), :], rsem.at[ACROSS_A])
     pair(0, PAIR_A)
 
@@ -332,13 +334,29 @@
                 send(col_slab(0, from_z), col_slab(0, from_z), THEN_Y, row_of(o, 0), c)
                 send(col_slab(1, from_y), col_slab(1, from_y), THEN_Z, row_of(0, o), c)
 
+    def row_slab(a, o):
+        at = pl.multiple_of(lax.rem(c + 2 * o, 8) * 64, 64)
+        return panels.at[a, pl.ds(at, 64), :]
+
     def rows_on():
-        done(panels.at[0, pl.ds(0, 384), :], rsem.at[ROWS])
+        done(panels.at[0, pl.ds(0, 256), :], rsem.at[ROWS])
+        for a, o in ((0, 3), (1, 1)):
+            send(row_slab(a, o), row_slab(a, o), ROWS_FAR, g, lax.rem(c + 8 - 2 * o, 8))
         for a in range(2):
-            for o in range(1, 4):
-                at = pl.multiple_of(lax.rem(c + 2 * o, 8) * 64, 64)
-                src = panels.at[a, pl.ds(at, 64), :]
-                send(src, src, ROWS_ON, g, other)
+            for o in (1, 3):
+                send(row_slab(a, o), row_slab(a, o), ROWS_ON, g, other)
+        send_parts(4, 8)
+
+    def rows_far_on():
+        done(panels.at[0, pl.ds(0, 128), :], rsem.at[ROWS_FAR])
+        for a in range(2):
+            send(row_slab(a, 2), row_slab(a, 2), ROWS_FAR_ON, g, other)
+
+    def rows_done():
+        done(panels.at[0, pl.ds(0, 128), :], rsem.at[ROWS_PAIR])
+        done(panels.at[0, pl.ds(0, 256), :], rsem.at[ROWS_ON])
+        done(panels.at[0, pl.ds(0, 128), :], rsem.at[ROWS_FAR_ON])
+        done(slab, lsem.at[L_ROWS])
 
     done(head.at[0, pl.ds(0, 256), :], rsem.at[PAIR_A])
 
@@ -409,28 +427,31 @@
     work[...] = head[2] - dot_tn(right, right)
     factor(1, lambda kb: None)
 
-    done(panels.at[0, pl.ds(0, 128), :], rsem.at[ROWS_PAIR])
-    done(panels.at[0, pl.ds(0, 384), :], rsem.at[ROWS_ON])
-    done(slab, lsem.at[L_ROWS])
     twelve = panels.at[pl.ds(0, 2), pl.ds(0, 384), :]
 
     def fetch(t, slot):
         return pltpu.make_async_copy(panels.at[t], inbuf.at[slot], lsem.at[L_IN + slot])
 
-    fetch(0, 0).start()
+    done(twelve, rsem.at[THEN_Y])
+    done(twelve, rsem.at[THEN_Z])
+    fetch(2, 0).start()
 
     @pl.loop(0, 6)
-    def _(t):
-        slot = lax.rem(t, 2)
-
-        @pl.when(t == 1)
-        def _():
-            done(twelve, rsem.at[THEN_Y])
-            done(twelve, rsem.at[THEN_Z])
-
-        @pl.when(t < 5)
-        def _():
-            fetch(t + 1, 1 - slot).start()
+    def _(step):
+        t = lax.rem(step + 2, 6)
+        slot = lax.rem(step, 2)
+
+        @pl.when(step == 2)
+        def _():
+            rows_far_on()
+
+        @pl.when(step == 3)
+        def _():
+            rows_done()
+
+        @pl.when(step < 5)
+        def _():
+            fetch(lax.rem(step + 3, 6), 1 - slot).start()
 
         fetch(t, slot).wait()
         first = dot_nt3(halves(inbuf[slot, :, :512]), (whigh[0], wlow[0]))
@@ -543,9 +564,11 @@
     done(head.at[1, pl.ds(0, 384), :], ssem.at[ACROSS_B])
     done(head.at[0, pl.ds(0, 256), :], ssem.at[PAIR_A])
     done(head.at[pl.ds(1, 2), pl.ds(0, 256), :], ssem.at[PAIR_B])
-    done(panels.at[0, pl.ds(0, 384), :], ssem.at[ROWS])
+    done(panels.at[0, pl.ds(0, 256), :], ssem.at[ROWS])
     done(panels.at[0, pl.ds(0, 128), :], ssem.at[ROWS_PAIR])
-    done(panels.at[0, pl.ds(0, 384), :], ssem.at[ROWS_ON])
+    done(panels.at[0, pl.ds(0, 256), :], ssem.at[ROWS_ON])
+    done(panels.at[0, pl.ds(0, 128), :], ssem.at[ROWS_FAR])
+    done(panels.at[0, pl.ds(0, 128), :], ssem.at[ROWS_FAR_ON])
 
     @pl.when(not_self)
     def _():
@@ -592,10 +615,40 @@
     )(rows)
 
 
+def place_kernel(src, dst, buf, sem):
+    def take(i):
+        return pltpu.make_async_copy(src.at[i // 4, pl.ds((i % 4) * 128, 128)], buf.at[i], sem.at[i])
+
+    def put(i):
+        return pltpu.make_async_copy(buf.at[i], dst.at[i // 4, pl.ds((i % 4) * 128, 128)],
+                                     sem.at[8 + i])
+
+    for i in range(8):
+        take(i).start()
+    for i in range(8):
+        take(i).wait()
+        put(i).start()
+    for i in range(8):
+        put(i).wait()
+
+
+def place_result(values):
+    anyspace = pl.BlockSpec(memory_space=pl.ANY)
+    return pl.pallas_call(
+        place_kernel,
+        out_shape=jax.ShapeDtypeStruct((2, 512, 16, 128), F32),
+        in_specs=[anyspace],
+        out_specs=anyspace,
+        scratch_shapes=[pltpu.VMEM((8, 128, 16, 128), F32), pltpu.SemaphoreType.DMA((16,))],
+        compiler_params=pltpu.CompilerParams(vmem_limit_bytes=56 * 1024 * 1024),
+        name="place",
+    )(values)
+
+
 def shards(kernel_rows):
     rows = kernel_rows.reshape(2, 64, 16384)
     out, _ = exchange(rows)
-    return out.reshape(2, 1, 512, 4, 1, 512)
+    return place_result(out).reshape(2, 1, 512, 4, 1, 512)
 
 
 def solution(mesh):

time: 164 us -> 158 us (0.963)
  local copies, waits for them, and re-layouts: 8.03 us -> 0 us
    unnamed x1 -> x0, local copies, waits for them, and re-layouts: 8.03 us -> none
    pallas_call x0 -> x1, Pallas kernels: none -> 6.42 us  [place_result(): pl.pallas_call(place_kernel, out_shape=jax.ShapeDtypeStruct((2, 512, 16,...]
    pallas_call x1, Pallas kernels: 156 us -> 150 us  [exchange(): pl.pallas_call(exchange_kernel, out_shape=(jax.ShapeDtypeStruct((2, 512,...]
where the time goes in v6:
time: 158 us; the launch traced here: 157 us
  Pallas kernels  156 us (99%)
    pallas_call x1, Pallas kernels, exchange(): pl.pallas_call(exchange_kernel, out_shape=(jax.ShapeDtypeStruct((2, 512,...  150 us
    pallas_call x1, Pallas kernels, place_result(): pl.pallas_call(place_kernel, out_shape=jax.ShapeDtypeStruct((2, 512, 16,...  6.42 us

profile of v6, /device:TPU:1, one launch (start us, length us, event | category | flops | bytes accessed | tf_op | source)
XLA Modules:
  0.0 156.7 jit_solution(3221708020911539069)
XLA Ops:
  0.0 150.1 %exchange.1 = (f32[2,512,16,128]{3,2,1,0:T(8,128)}, f32[6,512,1024]{2,1,0:T(8,128)}) custom-call(f32[2,64,16384]{2,1,0:T(8,128)} %bitcast.2), custom_call_target="tpu_custom_call" | custom-call | tf_op jit(solution)/shard_map/exchange/pallas_call | solution.py:586
  150.1 6.4 %place.1 = f32[2,512,16,128]{3,2,1,0:T(8,128)} custom-call(f32[2,512,16,128]{3,2,1,0:T(8,128)} %get-tuple-element.6.src), custom_call_target="tpu_custom_call" | custom-call | tf_op jit(solution)/shard_map/place/pallas_call | solution.py:637

commit v7 on v6

--- a/solution.py
+++ b/solution.py
@@ -500,14 +500,20 @@
         def _():
             leave(pair_no - 2, slot).wait()
 
+        special_row = (a == 0) & (g < 2)
+        special_col = (b == 0) & (c < 2)
+        plain = jnp.logical_not(special_row | special_col)
+
+        @pl.when(plain)
+        def _():
+            work[...] = dot_nt3((high[a], low[a]), (high[2 + b], low[2 + b]))
+
         done(tiles.at[n, pl.ds(0, 416), :], rsem.at[TILES + n])
         turn(n)
-        special_row = (a == 0) & (g < 2)
-        special_col = (b == 0) & (c < 2)
-
-        @pl.when(jnp.logical_not(special_row | special_col))
-        def _():
-            put(tiles[n] - dot_nt3((high[a], low[a]), (high[2 + b], low[2 + b])))
+
+        @pl.when(plain)
+        def _():
+            put(tiles[n] - work[...])
 
         @pl.when(special_col & jnp.logical_not(special_row) & (c == 0))
         def _():

time: 158 us -> 160 us (1.013)
  the two profiles are of different devices: /device:TPU:1 before, /device:TPU:10 now
where the time goes in v7:
time: 160 us
  Pallas kernels  160 us (100%)
    pallas_call x1, Pallas kernels, exchange(): pl.pallas_call(exchange_kernel, out_shape=(jax.ShapeDtypeStruct((2, 512,...  153 us
    pallas_call x1, Pallas kernels, place_result(): pl.pallas_call(place_kernel, out_shape=jax.ShapeDtypeStruct((2, 512, 16,...  6.42 us

profile of v7, /device:TPU:10, one launch (start us, length us, event | category | flops | bytes accessed | tf_op | source)
XLA Modules:
  0.0 159.8 jit_solution(9594381783519834510)
XLA Ops:
  0.0 153.2 %exchange.1 = (f32[2,512,16,128]{3,2,1,0:T(8,128)}, f32[6,512,1024]{2,1,0:T(8,128)}) custom-call(f32[2,64,16384]{2,1,0:T(8,128)} %bitcast.2), custom_call_target="tpu_custom_call" | custom-call | tf_op jit(solution)/shard_map/exchange/pallas_call | solution.py:592
  153.2 6.4 %place.1 = f32[2,512,16,128]{3,2,1,0:T(8,128)} custom-call(f32[2,512,16,128]{3,2,1,0:T(8,128)} %get-tuple-element.6.src), custom_call_target="tpu_custom_call" | custom-call | tf_op jit(solution)/shard_map/place/pallas_call | solution.py:643
